TPU v7x, 512 devices: a whole 4x4x16 slice. The times are simulated.
512 devices in a mesh: seq: 32 (over x_lo, z), head: 4 (over y), dp: 4 (over x_hi, core).
Axes of the slice: x: 4 (x_hi: 2, x_lo: 2; x = x_hi * 2 + x_lo), y: 4, z: 16, core: 2. Of those that a mesh axis runs over, the one named last changes fastest.
Arguments:
- layer_input: bfloat16 [4, 4096, 4096], P('dp', 'seq', 'head'), may hold values from -24 to 24
- head_input: bfloat16 [4, 4096, 4096], P('dp', 'seq', 'head'), may hold values from -6 to 6
- in_matrix: bfloat16 [4, 4096, 512], P('dp', 'seq', 'head'), may hold values from -6 to 6
- out_matrix: bfloat16 [4, 4096, 512], P('dp', 'seq', 'head'), may hold values from -6 to 6
- grad_output: bfloat16 [4, 4096, 4096], P('dp', 'seq', 'head'), may hold values from -0.59765625 to 0.59765625
- step_weight: bfloat16 [4096, 64], P(None, 'head'), may hold values from -0.09375 to 0.09375
- step_bias: float32 [64], P('head'), may hold values from -7 to -6
- decay_log: float32 [64], P('head'), may hold values from -6.22 to 2.78
Outputs:
- grad_heads: bfloat16 [4, 4096, 4096], P('dp', 'seq', 'head')
- grad_in_matrix: bfloat16 [4, 4096, 512], P('dp', 'seq', 'head')
- grad_out_matrix: bfloat16 [4, 4096, 512], P('dp', 'seq', 'head')
- grad_layer_input: bfloat16 [4, 4096, 4096], P('dp', 'seq', 'head')
- grad_step_weight: float32 [4096, 64], P(('seq', 'dp'), 'head')
All inputs are finite; a program needn't handle non-finite values.
Results may differ from a plain program's by a relative error of at most 0.02.
Values may be sent and summed in bfloat16 or wider, within the bound.
No kernel may reach another device: no remote copies, remote signals or barrier semaphores. Data moves between devices by JAX's collectives and lax.ppermute only.
A program may use at most 64 MiB of HBM per device.

v0:
```python
import jax
import jax.numpy as jnp
from jax import lax
from jax.sharding import PartitionSpec as P

H = 64
P_SIZE = 64
NSTATE = 128
G = 4
BLOCK = 128


PRECISION_LEVEL = lax.Precision.HIGHEST


def prefix(value, axis, join, neutral, backward):
    count = lax.axis_size(axis)
    place = lax.axis_index(axis)
    ahead = count - 1 - place if backward else place
    gathered = jax.tree.map(
        lambda a, kind: lax.all_gather(a.astype(kind), axis), value, (jnp.bfloat16, jnp.bfloat16)
    )
    state = jax.tree.map(lambda a, e: jnp.zeros_like(a) + jnp.asarray(e, a.dtype), value, neutral)

    def one(step, state):
        source = count - 1 - step if backward else step
        return join(
            state,
            jax.tree.map(
                lambda a, own: lax.dynamic_index_in_dim(a, source, 0, False).astype(own.dtype),
                gathered,
                value,
            ),
        )

    return lax.fori_loop(0, ahead, one, state)


def block_step(carry_state, inputs):
    input_block, b_block, c_block, step_block, decay_block = inputs
    cumulated = jnp.cumsum(decay_block, axis=-1)
    block_len = cumulated.shape[-1]
    lower_mask = jnp.arange(block_len)[:, None] >= jnp.arange(block_len)[None, :]
    decay_span = jnp.exp(
        jnp.where(lower_mask, cumulated[..., :, None] - cumulated[..., None, :], -1e30)
    )
    kernel = jnp.einsum("tgn,sgn->gts", c_block, b_block, precision=PRECISION_LEVEL)
    weight_values = kernel[:, None] * decay_span * step_block[..., None, :]
    within_block = jnp.einsum(
        "idwz,zidx->widx", weight_values, input_block, precision=PRECISION_LEVEL
    )
    carried = jnp.einsum("tgn,grnp->tgrp", c_block, carry_state, precision=PRECISION_LEVEL)
    output = within_block + jnp.moveaxis(jnp.exp(cumulated), -1, 0)[..., None] * carried
    totals = cumulated[..., -1]
    inflow = jnp.exp(totals[..., None] - cumulated) * step_block
    fresh_term = jnp.einsum(
        "grs,sgn,sgrp->grnp", inflow, b_block, input_block, precision=PRECISION_LEVEL
    )
    return (jnp.exp(totals)[..., None, None] * carry_state + fresh_term, output)


def segment(x_rows, b_rows, readout_rows, step_sizes, decays, start_state):
    length = x_rows.shape[0]
    blocks = length // BLOCK

    def split_rows(values):
        return values.reshape((blocks, BLOCK) + values.shape[1:])

    def split_last(values):
        return jnp.moveaxis(values.reshape(values.shape[:-1] + (blocks, BLOCK)), -2, 0)

    final_state, outputs = lax.scan(
        block_step,
        start_state,
        (
            split_rows(x_rows),
            split_rows(b_rows),
            split_rows(readout_rows),
            split_last(step_sizes),
            split_last(decays),
        ),
    )
    return (outputs.reshape(x_rows.shape), final_state)


def join_pairs(earlier, later):
    return (earlier[0] + later[0], jnp.exp(later[0])[..., None, None] * earlier[1] + later[1])


def body(
    layer_input, head_input, in_matrix, out_matrix, grad_output, step_weight, step_bias, decay_log
):
    tokens = head_input.shape[1]
    group_count = in_matrix.shape[2] // NSTATE
    ratio = H // G
    heads_here = group_count * ratio
    whole_input = lax.all_gather(layer_input, "head", axis=2, tiled=True)[0]
    preact = jnp.dot(whole_input, step_weight, preferred_element_type=jnp.float32) + step_bias
    step_sizes = jnp.transpose(jax.nn.softplus(preact)).reshape(group_count, ratio, tokens)
    rates = jnp.exp(decay_log).reshape(group_count, ratio)
    decays = -rates[..., None] * step_sizes
    x_rows = head_input[0].astype(jnp.float32).reshape(tokens, group_count, ratio, P_SIZE)
    b_rows = in_matrix[0].astype(jnp.float32).reshape(tokens, group_count, NSTATE)
    readout_rows = out_matrix[0].astype(jnp.float32).reshape(tokens, group_count, NSTATE)
    output_gradient = grad_output[0].astype(jnp.float32).reshape(tokens, group_count, ratio, P_SIZE)
    running_state = jnp.cumsum(decays, axis=-1)
    totals = running_state[..., -1]
    local_state = jnp.einsum(
        "grs,sgn,sgrp->grnp",
        jnp.exp(totals[..., None] - running_state) * step_sizes,
        b_rows,
        x_rows,
        precision=PRECISION_LEVEL,
    )
    local_grad = jnp.einsum(
        "vad,dvm,dvah->vamh",
        jnp.exp(running_state),
        readout_rows,
        output_gradient,
        precision=PRECISION_LEVEL,
    )
    neutral = (jnp.zeros_like(totals), jnp.zeros_like(local_state))
    incoming = prefix((totals, local_state), "seq", join_pairs, neutral, False)[1]
    outgoing = prefix((totals, local_grad), "seq", join_pairs, neutral, True)[1]

    def local_map(x_arg, b_arg, c_arg, step_arg):
        return segment(x_arg, b_arg, c_arg, step_arg, -rates[..., None] * step_arg, incoming)

    forward_out, pullback = jax.vjp(local_map, x_rows, b_rows, readout_rows, step_sizes)
    grad_x, grad_b, grad_c, grad_step = pullback((output_gradient, outgoing))
    grad_pre = (
        jnp.transpose(grad_step.reshape(heads_here, tokens)) * jax.nn.sigmoid(preact)
    ).astype(jnp.bfloat16)
    partial_terms = lax.dot_general(
        grad_pre, step_weight, (((1,), (1,)), ((), ())), preferred_element_type=jnp.float32
    )
    grad_input = lax.psum_scatter(
        partial_terms.astype(jnp.bfloat16), "head", scatter_dimension=1, tiled=True
    )
    grad_weight = lax.psum_scatter(
        lax.dot_general(
            whole_input, grad_pre, (((0,), (0,)), ((), ())), preferred_element_type=jnp.float32
        ),
        ("seq", "dp"),
        scatter_dimension=0,
        tiled=True,
    )
    return (
        grad_x.reshape(tokens, heads_here * P_SIZE).astype(jnp.bfloat16)[None],
        grad_b.reshape(tokens, group_count * NSTATE).astype(jnp.bfloat16)[None],
        grad_c.reshape(tokens, group_count * NSTATE).astype(jnp.bfloat16)[None],
        grad_input[None],
        grad_weight,
    )


def solution(mesh):
    in_specs = (
        P("dp", "seq", "head"),
        P("dp", "seq", "head"),
        P("dp", "seq", "head"),
        P("dp", "seq", "head"),
        P("dp", "seq", "head"),
        P(None, "head"),
        P("head"),
        P("head"),
    )
    out_specs = (
        P("dp", "seq", "head"),
        P("dp", "seq", "head"),
        P("dp", "seq", "head"),
        P("dp", "seq", "head"),
        P(("seq", "dp"), "head"),
    )
    return jax.shard_map(body, mesh=mesh, in_specs=in_specs, out_specs=out_specs, check_vma=False)
```

profile of v0, /device:TPU:1, one launch (start us, length us, event | category | flops | bytes accessed | tf_op | source)
XLA Modules:
  0.0 992.8 jit_solution(11479358953076989128)
XLA Ops:
  8.0 1.1 copy.110
  9.8 35.4 %all-gather.7.cloned.1.call-done = bf16[1,128,4096]{2,1,0:T(8,128)(2,1)} async-done(((bf16[1,128,1024]{2,1,0:T(8,128)(2,1)}), bf16[1,128,4096]{2,1,0:T(8,128)(2,1)}) %all-gather.7.cloned.1.call-update) | async-done | bytes 1048592 | tf_op jit(solution)/shard_map/all_gather | solution.py:97
  45.1 1.6 convolution_add_fusion.1
  47.4 1.9 fusion.5
  49.4 1.1 copy.101
  50.6 1.9 fusion.4
  53.5 52.3 %all-gather = bf16[32,16,1]{1,2,0:T(2,128)(2,1)S(1)} all-gather(bf16[1,16,1]{1,2,0:T(2,128)(2,1)S(1)} %slice.10), channel_id=2, replica_groups=mesh['seq'=32,'head'=4,'dp'=4] {'seq'}, dimensions={0}, use_global_device_ids=true | all-gather | bytes 1056 | tf_op jit(solution)/shard_map/all_gather | solution.py:21
  106.8 1.4 fusion.21
  110.4 69.1 %all-gather.11.cloned.1.call-done = bf16[32,16,128,64]{2,3,1,0:T(8,128)(2,1)} async-done(((bf16[1,16,128,64]{2,3,1,0:T(8,128)(2,1)}), bf16[32,16,128,64]{2,3,1,0:T(8,128)(2,1)}) %all-gather.11.cloned.1.call-update) | async-done | bytes 8388624 | tf_op jit(solution)/shard_map/all_gather | solution.py:21
  179.7 142.9 %all-gather.9.cloned.1.call-done = bf16[32,16,128,64]{2,3,1,0:T(8,128)(2,1)} async-done(((bf16[1,16,128,64]{2,3,1,0:T(8,128)(2,1)}), bf16[32,16,128,64]{2,3,1,0:T(8,128)(2,1)}) %all-gather.9.cloned.1.call-update) | async-done | bytes 8388624 | tf_op jit(solution)/shard_map/all_gather | solution.py:21
  322.7 68.7 %while.16 = (s32[]{:T(128)}, f32[1,16,128,64]{3,2,1,0:T(8,128)S(1)}, s32[]{:T(128)}, bf16[32,1,16]{2,1,0:T(2,128)(2,1)}, bf16[32,1,16,128,64]{3,4,2,0,1:T(8,128)...) while((s32[]{:T(128)}, f32[1,16,128,64]{3,2,1,0:T(8,128)S(1)}, s32[]{:T(128)}, ...), condition=%wide.region_2.3_spmd, body=%wide.region_1.2_spmd.sunk | while | flops 393238 | bytes 2359603 | solution.py:36
  391.4 2.6 fusion.22
  394.4 1.8 fusion.3
  397.9 1.0 fusion.38
  398.9 1.3 reduce_window_sum.30
  402.0 1.5 convolution_bitcast_fusion
  403.5 2.0 copy.143
  405.7 1.4 convolution_convert_fusion
  407.4 1.1 fusion.9
  409.2 1.9 fusion.2
  412.0 1.8 convolution_bitcast_fusion.4
  414.6 518.4 %reduce-scatter.7.cloned.1.call-done = f32[32,16]{1,0:T(8,128)} async-done(((f32[4096,16]{1,0:T(8,128)}), f32[32,16]{1,0:T(8,128)}) %reduce-scatter.7.cloned.1.call-update) | async-done | bytes 2064
  933.0 1.4 copy.144
  934.4 51.8 %reduce-scatter.5.cloned.1.call-done = bf16[128,1024]{1,0:T(8,128)(2,1)} async-done(((bf16[128,4096]{1,0:T(8,128)(2,1)}), bf16[128,1024]{1,0:T(8,128)(2,1)}) %reduce-scatter.5.cloned.1.call-update) | async-done | bytes 262160 | tf_op jit(solution)/shard_map/reduce_scatter | solution.py:137
  (199 shorter events, 80.8 us)
Async XLA Ops:
  7.2 38.0 %copy-start = (bf16[4096,16]{0,1:T(8,128)(2,1)S(1)}, bf16[4096,16]{0,1:T(8,128)(2,1)}, u32[]{:S(2)}) copy-start(bf16[4096,16]{0,1:T(8,128)(2,1)} %param.17) | copy-start | bytes 393220
  7.2 38.0 %all-gather.7.cloned.1.call-start = ((), (), s32[]{:S(2)}) async-start(), calls=%async_computation.2 | async-start | bytes 1310720 | tf_op jit(solution)/shard_map/all_gather | solution.py:97
  7.9 171.6 %all-gather.11.cloned.1.call-start = ((), (), s32[]{:S(2)}) async-start(), calls=%async_computation.5 | async-start | bytes 8650752 | tf_op jit(solution)/shard_map/all_gather | solution.py:21
  9.8 37.0 %copy-start.13 = (f32[16]{0:T(128)}, f32[16]{0:T(128)S(1)}, u32[]{:S(2)}) copy-start(f32[16]{0:T(128)S(1)} %exponential_negate_fusion) | copy-start | bytes 196
  46.8 2.6 copy-start.1
  47.3 132.2 %copy-start.2 = (f32[1,16,128]{1,2,0:T(8,128)}, f32[1,16,128]{1,2,0:T(8,128)S(1)}, u32[]{:S(2)}) copy-start(f32[1,16,128]{1,2,0:T(8,128)S(1)} %copy.97) | copy-start | bytes 24580
  49.4 273.2 %all-gather.9.cloned.1.call-start = ((), (), s32[]{:S(2)}) async-start(), calls=%async_computation.4 | async-start | bytes 8650752 | tf_op jit(solution)/shard_map/all_gather | solution.py:21
  52.5 880.5 %reduce-scatter.7.cloned.1.call-start = ((), (), s32[]{:S(2)}) async-start(), calls=%async_computation.6 | async-start | bytes 2113536
  52.6 127.1 %copy-start.9 = (pred[128,128]{1,0:T(8,128)(4,1)}, pred[128,128]{1,0:T(8,128)(4,1)S(1)}, u32[]{:S(2)}) copy-start(pred[128,128]{1,0:T(8,128)(4,1)S(1)} %iota_compare_fusion) | copy-start | bytes 49156
  53.5 126.1 %copy-start.6 = (f32[128,128]{1,0:T(8,128)}, f32[128,128]{1,0:T(8,128)S(1)}, u32[]{:S(2)}) copy-start(f32[128,128]{1,0:T(8,128)S(1)} %fusion.52) | copy-start | bytes 196612
  106.8 72.7 %copy-start.11 = (f32[16,128]{1,0:T(8,128)}, f32[16,128]{1,0:T(8,128)S(1)}, u32[]{:S(2)}) copy-start(f32[16,128]{1,0:T(8,128)S(1)} %copy.108) | copy-start | bytes 24580
  179.7 142.9 %copy-start.8 = (bf16[32,1,16]{2,1,0:T(2,128)(2,1)}, bf16[32,1,16]{2,1,0:T(2,128)(2,1)S(1)}, u32[]{:S(2)}) copy-start(bf16[32,1,16]{2,1,0:T(2,128)(2,1)S(1)} %get-tuple-element.524) | copy-start | bytes 3076
  391.4 15.7 %copy-start.4 = (bf16[1,128,128]{2,1,0:T(8,128)(2,1)S(1)}, bf16[1,128,128]{2,1,0:T(8,128)(2,1)}, u32[]{:S(2)}) copy-start(bf16[1,128,128]{2,1,0:T(8,128)(2,1)} %param.15) | copy-start | bytes 98308
  391.4 15.7 %copy-start.5 = (f32[128,128]{1,0:T(8,128)S(1)}, f32[128,128]{1,0:T(8,128)}, u32[]{:S(2)}) copy-start(f32[128,128]{1,0:T(8,128)} %get-tuple-element.363) | copy-start | bytes 196612
  391.4 17.8 %copy-start.7 = (f32[128,128]{1,0:T(8,128)S(1)}, f32[128,128]{1,0:T(8,128)}, u32[]{:S(2)}) copy-start(f32[128,128]{1,0:T(8,128)} %copy-done.6) | copy-start | bytes 196612
  391.4 17.8 %copy-start.10 = (pred[128,128]{1,0:T(8,128)(4,1)S(1)}, pred[128,128]{1,0:T(8,128)(4,1)}, u32[]{:S(2)}) copy-start(pred[128,128]{1,0:T(8,128)(4,1)} %copy-done.9) | copy-start | bytes 49156
  391.4 17.8 %copy-start.12 = (f32[16,128]{1,0:T(8,128)S(1)}, f32[16,128]{1,0:T(8,128)}, u32[]{:S(2)}) copy-start(f32[16,128]{1,0:T(8,128)} %copy-done.11) | copy-start | bytes 24580
  394.3 19.6 %copy-start.3 = (bf16[1,128,128]{2,1,0:T(8,128)(2,1)S(1)}, bf16[1,128,128]{2,1,0:T(8,128)(2,1)}, u32[]{:S(2)}) copy-start(bf16[1,128,128]{2,1,0:T(8,128)(2,1)} %param.14) | copy-start | bytes 98308
  405.5 580.8 %reduce-scatter.5.cloned.1.call-start = ((), (), s32[]{:S(2)}) async-start(), calls=%async_computation.3 | async-start | bytes 1310720 | tf_op jit(solution)/shard_map/reduce_scatter | solution.py:137
Sparse Core Ops, SparseCore 0:
  10.1 34.9 all-gather.6
  49.5 130.0 all-gather.10
  182.2 140.3 all-gather.8
  405.6 527.3 reduce-scatter.6
  936.3 49.9 reduce-scatter.4
where the time goes:
time: 996 us; the launch traced here: 993 us
  waiting for transfers between devices  818 us (82%)
  blocking collectives  52.3 us (5%)
  local copies, waits for them, and re-layouts  50.1 us (5%)
  other arithmetic  35.5 us (4%)
  matrix products  20.8 us (2%)
  between operations  14.1 us (1%)
    unnamed x6, waiting for transfers between devices  519 us
    all_gather x2, waiting for transfers between devices, prefix(): lax.all_gather(a.astype(kind), axis)  212 us
    all_gather x1, blocking collectives, prefix(): lax.all_gather(a.astype(kind), axis)  52.3 us
    reduce_scatter x1, waiting for transfers between devices, body(): lax.psum_scatter(partial_terms.astype(jnp.bfloat16), 'head', scatter_dime...  51.8 us
    dynamic_slice x62, local copies, waits for them, and re-layouts, one(): lax.dynamic_index_in_dim(a, source, 0, False).astype(own.dtype)  38.9 us
    all_gather x1, waiting for transfers between devices, body(): whole_input = lax.all_gather(layer_input, 'head', axis=2, tiled=True)[0]  35.4 us
    exp x31, other arithmetic, join_pairs(): jnp.exp(later[0])[..., None, None] * earlier[1] + later[1]  20.6 us
  transfers between devices with their start and end apart: 5, of which 5 were waited for; matrix products, arithmetic and copies ran while one was open for 2% of the time, Pallas kernels for 0%

commit v1 on v0

v1 whole, which is shorter than its diff:
```python
import jax
import jax.numpy as jnp
from jax import lax
from jax.experimental import pallas as pl
from jax.experimental.pallas import tpu as pltpu
from jax.sharding import PartitionSpec as P

P_SIZE = 64
NSTATE = 128
LANES = 128
EXTRA = 8
F32 = jnp.float32
BF16 = jnp.bfloat16
EXACT = lax.Precision.HIGHEST


def dot(a, b, ca, cb, precision=None):
    return lax.dot_general(
        a, b, (((ca,), (cb,)), ((), ())), preferred_element_type=F32, precision=precision
    )


def iota(shape, axis):
    return lax.broadcasted_iota(jnp.int32, shape, axis)


def halves(value):
    high = value.astype(BF16)
    return high, (value - high.astype(F32)).astype(BF16)


def segment_matrix(heads):
    shape = (heads, heads * P_SIZE)
    first = iota(shape, 0) * P_SIZE
    lane = iota(shape, 1)
    inside = jnp.logical_and(lane >= first, lane < first + P_SIZE)
    return jnp.where(inside, 1.0, 0.0).astype(BF16)


def expand(value, segments):
    high, low = halves(jnp.transpose(value))
    return dot(high, segments, 1, 0) + dot(low, segments, 1, 0)


def gather_heads(value, segments):
    high, low = halves(value)
    return dot(segments, high, 1, 1) + dot(segments, low, 1, 1)


def column(row):
    size = row.shape[1]
    diagonal = iota((size, size), 0) == iota((size, size), 1)
    return jnp.sum(jnp.where(diagonal, row, 0.0), axis=1, keepdims=True)


def pack_kernel(input_ref, weight_ref, out_ref):
    parts, _, width = out_ref.shape
    tokens = input_ref.shape[0]
    for part in range(parts):
        out_ref[part, :tokens, :] = input_ref[...]
        out_ref[part, tokens:, :] = weight_ref[:, part * width : (part + 1) * width]


def spread(shrink, states_ref, heads):
    slices, rows, _ = states_ref.shape
    first = shrink.astype(BF16).astype(F32)
    second = (shrink - first).astype(BF16).astype(F32)
    third = shrink - first - second
    place = iota((EXTRA, NSTATE), 0)
    each = slices // heads
    for head in range(heads):
        one = slice(head, head + 1)
        tile = jnp.where(place == 0, first[one], jnp.where(place == 1, second[one], third[one]))
        tile = jnp.where(place < 3, tile, 0.0).astype(BF16)
        for index in range(head * each, (head + 1) * each):
            states_ref[index, rows - EXTRA :, :] = tile


def state_kernel(
    whole_ref, weight_ref, bias_ref, log_ref, x_ref, b_ref, c_ref, g_ref,
    states_ref, small_ref, xs_ref, gs_ref,
):
    parts, _, width = whole_ref.shape
    heads = weight_ref.shape[0]
    tokens = x_ref.shape[0]
    slices = states_ref.shape[0]
    rows = heads * P_SIZE // slices
    preact = column(bias_ref[...])
    for part in range(parts):
        preact = preact + dot(
            weight_ref[:, part * width : (part + 1) * width], whole_ref[part, :tokens, :], 1, 1
        )
    tail = jnp.exp(-jnp.abs(preact))
    step = jnp.maximum(preact, 0.0) + jnp.log1p(tail)
    rate = jnp.exp(column(log_ref[...]))
    upto = jnp.where(iota((tokens, tokens), 0) <= iota((tokens, tokens), 1), 1.0, 0.0)
    cumulated = dot(-rate * step, upto, 1, 0, EXACT)
    total = cumulated[:, tokens - 1 :]
    small_ref[0] = preact
    small_ref[1] = step
    small_ref[2] = cumulated
    inflow = jnp.exp(total - cumulated) * step
    segments = segment_matrix(heads)
    scaled = (x_ref[...].astype(F32) * expand(inflow, segments)).astype(BF16)
    xs_ref[...] = scaled
    state = dot(scaled, b_ref[...], 0, 0).astype(BF16)
    states_ref[:, :rows, :] = state.reshape(slices, rows, NSTATE)
    scaled = (g_ref[...].astype(F32) * expand(jnp.exp(cumulated), segments)).astype(BF16)
    gs_ref[...] = scaled
    grad = dot(scaled, c_ref[...], 0, 0).astype(BF16)
    states_ref[:, rows : 2 * rows, :] = grad.reshape(slices, rows, NSTATE)
    spread(jnp.exp(total), states_ref, heads)


def scan_kernel(states_ref, out_ref):
    count, rows2, _ = out_ref.shape
    rows = rows2 // 2
    shrink = [
        jnp.sum(states_ref[place, rows2:, :].astype(F32), axis=0, keepdims=True)
        for place in range(count)
    ]
    for start, order in ((0, range(count)), (rows, reversed(range(count)))):
        state = jnp.zeros((rows, NSTATE), F32)
        for place in order:
            out_ref[place, start : start + rows, :] = state.astype(BF16)
            state = shrink[place] * state + states_ref[
                place, start : start + rows, :
            ].astype(F32)


def inner_kernel(small_ref, x_ref, b_ref, c_ref, g_ref, inner_ref, kernel_ref, sums_ref):
    _, heads, tokens = small_ref.shape
    cumulated = small_ref[2]
    kernel = dot(b_ref[...], c_ref[...], 1, 1)
    step_column = jnp.transpose(small_ref[1])
    cumulated_column = jnp.transpose(cumulated)
    allowed = iota((tokens, tokens), 0) <= iota((tokens, tokens), 1)
    lower = iota((tokens, LANES), 1) < P_SIZE
    zero = jnp.zeros((tokens, LANES), BF16)
    d_kernel = jnp.zeros((tokens, tokens), F32)
    row_sums = []
    products = []
    for pair in range(heads // 2):
        lanes = slice(pair * LANES, (pair + 1) * LANES)
        x = x_ref[:, lanes]
        g = g_ref[:, lanes]
        both = []
        for half in range(2):
            head = 2 * pair + half
            span = cumulated[head : head + 1, :] - cumulated_column[:, head : head + 1]
            span = jnp.exp(jnp.where(allowed, span, -1e30))
            mine = jnp.where(lower, x, zero) if half == 0 else jnp.where(lower, zero, x)
            product = dot(mine, g, 1, 1) * span * step_column[:, head : head + 1]
            d_kernel = d_kernel + product
            row_sums.append(jnp.sum(product * kernel, axis=0, keepdims=True))
            both.append(dot((span * kernel).astype(BF16), g, 1, 0))
        inner = jnp.where(lower, both[0], both[1])
        inner_ref[:, lanes] = inner
        products.append(x.astype(F32) * inner)
    kernel_ref[...] = d_kernel.astype(BF16)
    sums_ref[0] = jnp.concatenate(row_sums, axis=0)
    sums_ref[1] = gather_heads(jnp.concatenate(products, axis=1), segment_matrix(heads))


def last_kernel(
    states_ref, small_ref, log_ref, inner_ref, kernel_ref, sums_ref,
    x_ref, b_ref, c_ref, g_ref, xs_ref, gs_ref, whole_ref,
    gx_ref, gb_ref, gc_ref, pre_ref, part_ref,
):
    _, heads, tokens = small_ref.shape
    preact = small_ref[0]
    step = small_ref[1]
    cumulated = small_ref[2]
    total = cumulated[:, tokens - 1 :]
    rate = jnp.exp(column(log_ref[...]))
    left = jnp.exp(total - cumulated)
    segments = segment_matrix(heads)
    rows = states_ref.shape[1] // 2
    state = states_ref[:, :rows, :].reshape(heads * P_SIZE, NSTATE)
    grad = states_ref[:, rows:, :].reshape(heads * P_SIZE, NSTATE)
    x = x_ref[...].astype(F32)
    from_grad = dot(b_ref[...], grad, 1, 1)
    from_state = dot(c_ref[...], state, 1, 1)
    readout = jnp.exp(cumulated) * gather_heads(g_ref[...].astype(F32) * from_state, segments)
    gx_ref[...] = (
        expand(step, segments) * (inner_ref[...] + expand(left, segments) * from_grad)
    ).astype(BF16)
    inflow_part = left * gather_heads(x * from_grad, segments)
    direct = sums_ref[1] + inflow_part
    high, low = halves(state.astype(F32) * grad.astype(F32))
    meeting = jnp.sum(dot(segments, high, 1, 0) + dot(segments, low, 1, 0), axis=1, keepdims=True)
    of_total = jnp.sum(step * inflow_part, axis=1, keepdims=True) + jnp.exp(total) * meeting
    of_cumulated = sums_ref[0] + readout - step * direct
    onward = jnp.where(iota((tokens, tokens), 0) >= iota((tokens, tokens), 1), 1.0, 0.0)
    of_decay = dot(of_cumulated, onward, 1, 0, EXACT) + of_total
    grad_step = direct - rate * of_decay
    sigmoid = 1.0 / (1.0 + jnp.exp(-preact))
    grad_pre = (grad_step * sigmoid).astype(BF16)
    gb_ref[...] = (
        dot(kernel_ref[...], c_ref[...], 1, 0) + dot(xs_ref[...], grad, 1, 0)
    ).astype(BF16)
    gc_ref[...] = (
        dot(kernel_ref[...], b_ref[...], 0, 0) + dot(gs_ref[...], state, 1, 0)
    ).astype(BF16)
    pre_ref[...] = grad_pre
    per = part_ref.shape[1]
    shards = heads // per
    size = LANES // shards
    shape = (heads, heads)
    swapped = iota(shape, 1) == shards * (iota(shape, 0) % per) + iota(shape, 0) // per
    swapped = dot(jnp.where(swapped, 1.0, 0.0).astype(BF16), grad_pre, 1, 0).astype(BF16)
    group = 8 // per
    block = iota((8, LANES), 1) // size
    row = iota((8, LANES), 0) // per
    masks = [
        jnp.logical_and(block == index, row == index % group) for index in range(shards)
    ]
    parts, _, width = whole_ref.shape
    for part in range(parts):
        term = dot(swapped, whole_ref[part, :tokens, :], 1, 0)
        for index in range(width // LANES):
            lanes = slice(index * LANES, (index + 1) * LANES)
            turned = []
            for first in range(0, heads, 8):
                piece = term[first : first + 8, lanes]
                turned.append(
                    [piece] + [pltpu.roll(piece, size * turn, 1) for turn in range(1, shards)]
                )
            for shard in range(shards):
                packed = jnp.zeros((8, LANES), F32)
                for index2 in range(shards):
                    source = turned[index2 // group][(index2 - shard) % shards]
                    packed = jnp.where(masks[index2], source, packed)
                total_rows = packed[:per]
                for other in range(1, group):
                    total_rows = total_rows + packed[other * per : (other + 1) * per]
                where = (part * (width // LANES) + index) * shards + shard
                part_ref[where] = total_rows.astype(part_ref.dtype)


def input_kernel(place_ref, whole_ref, *refs):
    out_ref = refs[-1]
    parts = whole_ref.shape[0]
    tokens = out_ref.shape[0]
    pre = jnp.concatenate([ref[...] for ref in refs[:-1]], axis=0)
    weight = jnp.concatenate(
        [whole_ref[lax.rem(place_ref[0] + parts - shift, parts), tokens:, :] for shift in range(parts)],
        axis=0,
    )
    out_ref[...] = dot(pre, weight, 0, 0).astype(BF16)


def sum_kernel(part_ref, out_ref):
    heads, size = out_ref.shape
    total = jnp.sum(part_ref[...].astype(F32), axis=0)
    per = total.shape[0]
    shards = heads // per
    for shard in range(shards):
        piece = total[:, shard * size : (shard + 1) * size]
        for row in range(per):
            head = row * shards + shard
            out_ref[head : head + 1, :] = piece[row : row + 1, :]


def call(kernel, out_shape, *args, micros=2, scalars=0):
    cost = pl.CostEstimate(flops=0, transcendentals=0, bytes_accessed=micros * 3_000_000)
    specs = [pl.BlockSpec(memory_space=pltpu.SMEM)] * scalars
    specs += [pl.BlockSpec(memory_space=pltpu.VMEM)] * (len(args) - scalars)
    return pl.pallas_call(
        kernel, out_shape=out_shape, in_specs=specs, name=kernel.__name__, cost_estimate=cost
    )(*args)


def exchange(value, axis):
    return lax.all_to_all(value, axis, 0, 0, tiled=True)


def body(
    layer_input, head_input, in_matrix, out_matrix, grad_output, step_weight, step_bias, decay_log
):
    parts = lax.axis_size("head")
    places = lax.axis_size("seq")
    shards = lax.axis_size("dp")
    tokens, width = layer_input.shape[1:]
    heads = step_weight.shape[1]
    rows = heads * P_SIZE // places
    shape = jax.ShapeDtypeStruct
    x, b, c, g = head_input[0], in_matrix[0], out_matrix[0], grad_output[0]
    weight = step_weight.T
    bias = step_bias.reshape(1, heads)
    logs = decay_log.reshape(1, heads)
    packed = call(
        pack_kernel, shape((parts, tokens + heads, width), BF16), layer_input[0], weight
    )
    whole = exchange(packed, "head")
    states, small, xs, gs = call(
        state_kernel,
        (
            shape((places, 2 * rows + EXTRA, NSTATE), BF16),
            shape((3, heads, tokens), F32),
            shape(x.shape, BF16),
            shape(x.shape, BF16),
        ),
        whole, weight, bias, logs, x, b, c, g,
    )
    states = exchange(states, "seq")
    inner, kernel, sums = call(
        inner_kernel,
        (shape(x.shape, F32), shape((tokens, tokens), BF16), shape((2, heads, tokens), F32)),
        small, x, b, c, g,
    )
    states = call(scan_kernel, shape((places, 2 * rows, NSTATE), BF16), states)
    states = exchange(states, "seq")
    grad_x, grad_b, grad_c, pre, part = call(
        last_kernel,
        (
            shape(x.shape, BF16),
            shape(b.shape, BF16),
            shape(c.shape, BF16),
            shape((heads, tokens), BF16),
            shape((places * shards, heads // shards, LANES), BF16),
        ),
        states, small, logs, inner, kernel, sums, x, b, c, g, xs, gs, whole,
    )
    part = exchange(part, ("seq", "dp"))
    others = [
        lax.ppermute(pre, "head", [(i, (i + shift) % parts) for i in range(parts)])
        for shift in range(1, parts)
    ]
    place = lax.axis_index("head").astype(jnp.int32).reshape(1)
    grad_input = call(
        input_kernel, shape((tokens, width), BF16), place, whole, pre, *others, scalars=1
    )
    term = call(sum_kernel, shape((heads, LANES // shards), F32), part)
    return (grad_x[None], grad_b[None], grad_c[None], grad_input[None], term.T)


def solution(mesh):
    in_specs = (P("dp", "seq", "head"),) * 5 + (P(None, "head"), P("head"), P("head"))
    out_specs = (P("dp", "seq", "head"),) * 4 + (P(("seq", "dp"), "head"),)
    return jax.shard_map(body, mesh=mesh, in_specs=in_specs, out_specs=out_specs, check_vma=False)
```

time: 996 us -> 150 us (0.15)
  waiting for transfers between devices: 818 us -> 31.4 us
  local copies, waits for them, and re-layouts: 50.1 us -> 2.06 us
  other arithmetic: 35.5 us -> 0 us
  starting transfers between devices: 0.38 us -> 26.4 us
  matrix products: 20.8 us -> 0 us
  Pallas kernels: 0 us -> 19.9 us
  blocking collectives: 52.3 us -> 68.3 us
  between operations: 14.1 us -> 0.72 us
    unnamed x6 -> x0, waiting for transfers between devices: 519 us -> none
    all_gather x3 -> x0, waiting for transfers between devices: 247 us -> none  [the longest x2 212 us: prefix(): lax.all_gather(a.astype(kind), axis)]
    all_to_all x0 -> x2, blocking collectives: none -> 68.3 us  [exchange(): return lax.all_to_all(value, axis, 0, 0, tiled=True)]
    all_gather x1 -> x0, blocking collectives: 52.3 us -> none  [prefix(): lax.all_gather(a.astype(kind), axis)]
    reduce_scatter x1 -> x0, waiting for transfers between devices: 51.8 us -> none  [body(): lax.psum_scatter(partial_terms.astype(jnp.bfloat16), 'head', scatter_dime...]
    dynamic_slice x62 -> x0, local copies, waits for them, and re-layouts: 38.9 us -> none  [one(): lax.dynamic_index_in_dim(a, source, 0, False).astype(own.dtype)]
    all_to_all x0 -> x2, waiting for transfers between devices: none -> 29.1 us  [exchange(): return lax.all_to_all(value, axis, 0, 0, tiled=True)]
    dot_general x14 -> x0, matrix products: 20.8 us -> none  [the longest x2 3.65 us: block_step(): jnp.einsum('grs,sgn,sgrp->grnp', inflow, b_block, input_block, precision=...]
  transfers between devices with their start and end apart: 5 -> 5, of which waited for: 5 -> 3; matrix products, arithmetic and copies ran while one was open for 2% -> 0% of each run, Pallas kernels for 0% -> 3%
where the time goes in v1:
time: 150 us; the launch traced here: 149 us
  blocking collectives  68.3 us (46%)
  waiting for transfers between devices  31.4 us (21%)
  starting transfers between devices  26.4 us (18%)
  Pallas kernels  19.9 us (13%)
  local copies, waits for them, and re-layouts  2.06 us (1%)
    all_to_all x2, blocking collectives, exchange(): return lax.all_to_all(value, axis, 0, 0, tiled=True)  68.3 us
    all_to_all x2, waiting for transfers between devices, exchange(): return lax.all_to_all(value, axis, 0, 0, tiled=True)  29.1 us
    pallas_call x7, Pallas kernels, call(): pl.pallas_call(kernel, out_shape=out_shape, in_specs=specs, name=kernel._...  19.9 us
    all_to_all x2, starting transfers between devices, exchange(): return lax.all_to_all(value, axis, 0, 0, tiled=True)  18 us
    ppermute x3, starting transfers between devices, body(): lax.ppermute(pre, 'head', [(i, (i + shift) % parts) for i in range(parts)])  8.41 us
  transfers between devices with their start and end apart: 5, of which 3 were waited for; matrix products, arithmetic and copies ran while one was open for 0% of the time, Pallas kernels for 3%

profile of v1, /device:TPU:1, one launch (start us, length us, event | category | flops | bytes accessed | tf_op | source)
XLA Modules:
  0.0 148.9 jit_solution(12983371667688270748)
XLA Ops:
  0.6 2.1 %pack_kernel.1 = bf16[4,144,1024]{2,1,0:T(8,128)(2,1)} custom-call(bf16[128,1024]{1,0:T(8,128)(2,1)} %bitcast.28, bf16[16,4096]{1,0:T(8,128)(2,1)} %bitcast.20), custom_call_target="tpu_custom_call" | custom-call | bytes 6000000 | tf_op jit(solution)/shard_map/pack_kernel/pallas_call | solution.py:269
  2.7 15.6 %all_to_all.20.whole_ref = bf16[4,144,1024]{2,1,0:T(8,128)(2,1)} all-to-all(bf16[4,144,1024]{2,1,0:T(8,128)(2,1)} %pack_kernel.1), channel_id=1, replica_groups=mesh['seq'=32,'head'=4,'dp'=4] {'head'}, dimensions={0} | all-to-all | bytes 2359296 | tf_op jit(solution)/shard_map/all_to_all | solution.py:275
  18.3 4.6 %state_kernel.1 = (bf16[32,72,128]{2,1,0:T(8,128)(2,1)}, f32[3,16,128]{2,1,0:T(8,128)}, bf16[128,1024]{1,0:T(8,128)(2,1)}, bf16[128,1024]{1,0:T(8,128)(2,1)}) custom-call(bf16[4,144,1024]{2,1,0:T(8,128)(2,1)} %all_to_all.20.whole_ref, bf16[16,4096]{1,0:T(8,128)(2,1)} %bitcast.21, f32[1,16]{1,0:T(1,128)} %bitcast.33, f32[1,16]{1,0:T(1,128)} %bitcast.31, ...), custom_call_target="tpu_custom_call" | custom-call | bytes 6000000 | tf_op jit(solution)/shard_map/state_kernel/pallas_call | solution.py:269
  22.8 52.8 %all_to_all.21.states_ref = bf16[32,72,128]{2,1,0:T(8,128)(2,1)} all-to-all(bf16[32,72,128]{2,1,0:T(8,128)(2,1)} %get-tuple-element.17), channel_id=1, replica_groups=mesh['seq'=32,'head'=4,'dp'=4] {'seq'}, dimensions={0} | all-to-all | bytes 1179648 | tf_op jit(solution)/shard_map/all_to_all | solution.py:275
  75.6 2.0 %scan_kernel.1 = bf16[32,64,128]{2,1,0:T(8,128)(2,1)} custom-call(bf16[32,72,128]{2,1,0:T(8,128)(2,1)} %all_to_all.21.states_ref), custom_call_target="tpu_custom_call" | custom-call | bytes 6000000 | tf_op jit(solution)/shard_map/scan_kernel/pallas_call | solution.py:269
  77.6 7.4 %all-to-all-start.2 = ((bf16[32,64,128]{2,1,0:T(8,128)(2,1)}), bf16[32,64,128]{2,1,0:T(8,128)(2,1)S(1)}, u32[]{:S(2)}, u32[]{:S(2)}) async-start(bf16[32,64,128]{2,1,0:T(8,128)(2,1)} %scan_kernel.1), calls=%async_computation.2 | async-start | bytes 1048576 | tf_op jit(solution)/shard_map/all_to_all | solution.py:275
  85.1 2.8 %inner_kernel.1 = (f32[128,1024]{1,0:T(8,128)}, bf16[128,128]{1,0:T(8,128)(2,1)}, f32[2,16,128]{2,1,0:T(8,128)}) custom-call(f32[3,16,128]{2,1,0:T(8,128)} %get-tuple-element.18.small_ref, bf16[128,1024]{1,0:T(8,128)(2,1)} %bitcast.15, bf16[128,128]{1,0:T(8,128)(2,1)} %bitcast.23, bf16[128,128]{1,0:T(8,128)(2,1)} %bitcast.26, bf16[128,1024]{1,0:T(8,128)(2,1)} %bitcast.18), custom_call_target="tpu_custom_call" | custom-call | bytes 6000000 | tf_op jit(solution)/shard_map/inner_kernel/pallas_call | solution.py:269
  87.9 27.0 %all-to-all-done.2.states_ref = bf16[32,64,128]{2,1,0:T(8,128)(2,1)S(1)} async-done(((bf16[32,64,128]{2,1,0:T(8,128)(2,1)}), bf16[32,64,128]{2,1,0:T(8,128)(2,1)S(1)}, u32[]{:S(2)}, u32[]{:S(2)}) %all-to-all-start.2) | async-done | bytes 524320 | tf_op jit(solution)/shard_map/all_to_all | solution.py:275
  115.0 0.8 copy-done
  115.8 4.5 %last_kernel.1 = (bf16[128,1024]{1,0:T(8,128)(2,1)}, bf16[128,128]{1,0:T(8,128)(2,1)}, bf16[128,128]{1,0:T(8,128)(2,1)}, bf16[16,128]{1,0:T(8,128)(2,1)}, bf16[128,4,128]{2,1,0:T(4,128)(2,1)}) custom-call(bf16[32,64,128]{2,1,0:T(8,128)(2,1)} %copy-done, f32[3,16,128]{2,1,0:T(8,128)} %get-tuple-element.18.small_ref, f32[1,16]{1,0:T(1,128)} %bitcast.32, ...), custom_call_target="tpu_custom_call" | custom-call | bytes 6000000 | tf_op jit(solution)/shard_map/last_kernel/pallas_call | solution.py:269
  120.3 10.6 %all-to-all-start.3 = ((bf16[128,4,128]{2,1,0:T(4,128)(2,1)}), bf16[128,4,128]{2,1,0:T(4,128)(2,1)S(1)}, u32[]{:S(2)}, u32[]{:S(2)}) async-start(bf16[128,4,128]{2,1,0:T(4,128)(2,1)} %get-tuple-element.28), calls=%async_computation.3 | async-start | bytes 262144 | tf_op jit(solution)/shard_map/all_to_all | solution.py:275
  130.9 2.0 %collective-permute-start = (bf16[16,128]{1,0:T(8,128)(2,1)}, bf16[16,128]{1,0:T(8,128)(2,1)S(1)}, u32[]{:S(2)}, u32[]{:S(2)}) collective-permute-start(bf16[16,128]{1,0:T(8,128)(2,1)} %get-tuple-element.27.refs_0_), channel_id=1, source_target_pairs={{0,4},{4,8},{8,12},{12,0},{1,5},{5,9},{9,13},{13,1},{2,6},{6,10},{... | collective-permute-start | bytes 12296 | tf_op jit(solution)/shard_map/ppermute | solution.py:327
  132.9 3.9 %collective-permute-start.1 = (bf16[16,128]{1,0:T(8,128)(2,1)}, bf16[16,128]{1,0:T(8,128)(2,1)S(1)}, u32[]{:S(2)}, u32[]{:S(2)}) collective-permute-start(bf16[16,128]{1,0:T(8,128)(2,1)} %get-tuple-element.27.refs_0_), channel_id=1, source_target_pairs={{0,8},{4,12},{8,0},{12,4},{1,9},{5,13},{9,1},{13,5},{2,10},{6,14},... | collective-permute-start | bytes 12296 | tf_op jit(solution)/shard_map/ppermute | solution.py:327
  136.7 2.5 %collective-permute-start.2 = (bf16[16,128]{1,0:T(8,128)(2,1)}, bf16[16,128]{1,0:T(8,128)(2,1)S(1)}, u32[]{:S(2)}, u32[]{:S(2)}) collective-permute-start(bf16[16,128]{1,0:T(8,128)(2,1)} %get-tuple-element.27.refs_0_), channel_id=1, source_target_pairs={{0,12},{4,0},{8,4},{12,8},{1,13},{5,1},{9,5},{13,9},{2,14},{6,2},{... | collective-permute-start | bytes 12296 | tf_op jit(solution)/shard_map/ppermute | solution.py:327
  139.3 0.0 collective-permute-done.refs_1_
  139.3 0.0 copy-start.2
  139.3 0.0 collective-permute-done.1.refs_2_
  139.3 2.3 %collective-permute-done.2.refs_3_ = bf16[16,128]{1,0:T(8,128)(2,1)S(1)} collective-permute-done((bf16[16,128]{1,0:T(8,128)(2,1)}, bf16[16,128]{1,0:T(8,128)(2,1)S(1)}, u32[]{:S(2)}, u32[]{:S(2)}) %collective-permute-start.2) | collective-permute-done | bytes 4128 | tf_op jit(solution)/shard_map/ppermute | solution.py:327
  141.6 0.0 copy-done.3
  141.6 0.6 copy-done.4
  142.2 2.2 %input_kernel.1 = bf16[128,1024]{1,0:T(8,128)(2,1)} custom-call(s32[1]{0:T(128)} %bitcast.11.place_ref, bf16[4,144,1024]{2,1,0:T(8,128)(2,1)} %all_to_all.20.whole_ref, bf16[16,128]{1,0:T(8,128)(2,1)} %get-tuple-element.27.refs_0_, bf16[16,128]{1,0:T(8,128)(2,1)} %copy-done.2, bf16[16,128]{1,0:T(8,128)(2,1)} %copy-done.3, bf16[16,128]{1,0:T(8,128)(2,1)} %copy-done.4), custom_call_target="tpu_custom_call" | custom-call | bytes 6000000 | tf_op jit(solution)/shard_map/input_kernel/pallas_call | solution.py:269
  144.4 2.1 %all-to-all-done.3.part_ref = bf16[128,4,128]{2,1,0:T(4,128)(2,1)S(1)} async-done(((bf16[128,4,128]{2,1,0:T(4,128)(2,1)}), bf16[128,4,128]{2,1,0:T(4,128)(2,1)S(1)}, u32[]{:S(2)}, u32[]{:S(2)}) %all-to-all-start.3) | async-done | bytes 131104 | tf_op jit(solution)/shard_map/all_to_all | solution.py:275
  146.5 0.6 copy-done.1
  147.2 1.7 %sum_kernel.1 = f32[16,32]{1,0:T(8,128)} custom-call(bf16[128,4,128]{2,1,0:T(4,128)(2,1)} %copy-done.1), custom_call_target="tpu_custom_call" | custom-call | bytes 6000000 | tf_op jit(solution)/shard_map/sum_kernel/pallas_call | solution.py:269
  (5 shorter events, 0.0 us)
Async XLA Ops:
  77.6 37.3 %all-to-all-start.2 = ((bf16[32,64,128]{2,1,0:T(8,128)(2,1)}), bf16[32,64,128]{2,1,0:T(8,128)(2,1)S(1)}, u32[]{:S(2)}, u32[]{:S(2)}) async-start(bf16[32,64,128]{2,1,0:T(8,128)(2,1)} %scan_kernel.1), calls=%async_computation.2 | async-start | bytes 1048576 | tf_op jit(solution)/shard_map/all_to_all | solution.py:275
  115.0 0.8 copy-start
  120.3 26.3 %all-to-all-start.3 = ((bf16[128,4,128]{2,1,0:T(4,128)(2,1)}), bf16[128,4,128]{2,1,0:T(4,128)(2,1)S(1)}, u32[]{:S(2)}, u32[]{:S(2)}) async-start(bf16[128,4,128]{2,1,0:T(4,128)(2,1)} %get-tuple-element.28), calls=%async_computation.3 | async-start | bytes 262144 | tf_op jit(solution)/shard_map/all_to_all | solution.py:275
  130.9 8.4 %collective-permute-start = (bf16[16,128]{1,0:T(8,128)(2,1)}, bf16[16,128]{1,0:T(8,128)(2,1)S(1)}, u32[]{:S(2)}, u32[]{:S(2)}) collective-permute-start(bf16[16,128]{1,0:T(8,128)(2,1)} %get-tuple-element.27.refs_0_), channel_id=1, source_target_pairs={{0,4},{4,8},{8,12},{12,0},{1,5},{5,9},{9,13},{13,1},{2,6},{6,10},{... | collective-permute-start | bytes 12296 | tf_op jit(solution)/shard_map/ppermute | solution.py:327
  132.9 6.5 %collective-permute-start.1 = (bf16[16,128]{1,0:T(8,128)(2,1)}, bf16[16,128]{1,0:T(8,128)(2,1)S(1)}, u32[]{:S(2)}, u32[]{:S(2)}) collective-permute-start(bf16[16,128]{1,0:T(8,128)(2,1)} %get-tuple-element.27.refs_0_), channel_id=1, source_target_pairs={{0,8},{4,12},{8,0},{12,4},{1,9},{5,13},{9,1},{13,5},{2,10},{6,14},... | collective-permute-start | bytes 12296 | tf_op jit(solution)/shard_map/ppermute | solution.py:327
  136.7 4.9 %collective-permute-start.2 = (bf16[16,128]{1,0:T(8,128)(2,1)}, bf16[16,128]{1,0:T(8,128)(2,1)S(1)}, u32[]{:S(2)}, u32[]{:S(2)}) collective-permute-start(bf16[16,128]{1,0:T(8,128)(2,1)} %get-tuple-element.27.refs_0_), channel_id=1, source_target_pairs={{0,12},{4,0},{8,4},{12,8},{1,13},{5,1},{9,5},{13,9},{2,14},{6,2},{... | collective-permute-start | bytes 12296 | tf_op jit(solution)/shard_map/ppermute | solution.py:327
  139.3 2.3 %copy-start.2 = (bf16[16,128]{1,0:T(8,128)(2,1)}, bf16[16,128]{1,0:T(8,128)(2,1)S(1)}, u32[]{:S(2)}) copy-start(bf16[16,128]{1,0:T(8,128)(2,1)S(1)} %collective-permute-done.refs_1_) | copy-start | bytes 12292
  139.3 2.3 %copy-start.3 = (bf16[16,128]{1,0:T(8,128)(2,1)}, bf16[16,128]{1,0:T(8,128)(2,1)S(1)}, u32[]{:S(2)}) copy-start(bf16[16,128]{1,0:T(8,128)(2,1)S(1)} %collective-permute-done.1.refs_2_) | copy-start | bytes 12292
  141.6 0.6 copy-start.4
  146.5 0.7 copy-start.1

commit v2 on v1

--- a/solution.py
+++ b/solution.py
@@ -262,17 +262,22 @@
             out_ref[head : head + 1, :] = piece[row : row + 1, :]
 
 
+def inside(value):
+    return pltpu.with_memory_space_constraint(value, pltpu.VMEM)
+
+
 def call(kernel, out_shape, *args, micros=2, scalars=0):
     cost = pl.CostEstimate(flops=0, transcendentals=0, bytes_accessed=micros * 3_000_000)
     specs = [pl.BlockSpec(memory_space=pltpu.SMEM)] * scalars
     specs += [pl.BlockSpec(memory_space=pltpu.VMEM)] * (len(args) - scalars)
     return pl.pallas_call(
-        kernel, out_shape=out_shape, in_specs=specs, name=kernel.__name__, cost_estimate=cost
+        kernel, out_shape=out_shape, in_specs=specs, name=kernel.__name__, cost_estimate=cost,
+        compiler_params=pltpu.CompilerParams(vmem_limit_bytes=32 * 2**20),
     )(*args)
 
 
 def exchange(value, axis):
-    return lax.all_to_all(value, axis, 0, 0, tiled=True)
+    return inside(lax.all_to_all(value, axis, 0, 0, tiled=True))
 
 
 def body(
@@ -285,31 +290,32 @@
     heads = step_weight.shape[1]
     rows = heads * P_SIZE // places
     shape = jax.ShapeDtypeStruct
+    near = pltpu.VMEM
     x, b, c, g = head_input[0], in_matrix[0], out_matrix[0], grad_output[0]
     weight = step_weight.T
     bias = step_bias.reshape(1, heads)
     logs = decay_log.reshape(1, heads)
     packed = call(
-        pack_kernel, shape((parts, tokens + heads, width), BF16), layer_input[0], weight
+        pack_kernel, near((parts, tokens + heads, width), BF16), layer_input[0], weight
     )
     whole = exchange(packed, "head")
     states, small, xs, gs = call(
         state_kernel,
         (
-            shape((places, 2 * rows + EXTRA, NSTATE), BF16),
-            shape((3, heads, tokens), F32),
-            shape(x.shape, BF16),
-            shape(x.shape, BF16),
+            near((places, 2 * rows + EXTRA, NSTATE), BF16),
+            near((3, heads, tokens), F32),
+            near(x.shape, BF16),
+            near(x.shape, BF16),
         ),
         whole, weight, bias, logs, x, b, c, g,
     )
     states = exchange(states, "seq")
     inner, kernel, sums = call(
         inner_kernel,
-        (shape(x.shape, F32), shape((tokens, tokens), BF16), shape((2, heads, tokens), F32)),
+        (near(x.shape, F32), near((tokens, tokens), BF16), near((2, heads, tokens), F32)),
         small, x, b, c, g,
     )
-    states = call(scan_kernel, shape((places, 2 * rows, NSTATE), BF16), states)
+    states = call(scan_kernel, near((places, 2 * rows, NSTATE), BF16), states)
     states = exchange(states, "seq")
     grad_x, grad_b, grad_c, pre, part = call(
         last_kernel,
@@ -317,14 +323,14 @@
             shape(x.shape, BF16),
             shape(b.shape, BF16),
             shape(c.shape, BF16),
-            shape((heads, tokens), BF16),
-            shape((places * shards, heads // shards, LANES), BF16),
+            near((heads, tokens), BF16),
+            near((places * shards, heads // shards, LANES), BF16),
         ),
         states, small, logs, inner, kernel, sums, x, b, c, g, xs, gs, whole,
     )
     part = exchange(part, ("seq", "dp"))
     others = [
-        lax.ppermute(pre, "head", [(i, (i + shift) % parts) for i in range(parts)])
+        inside(lax.ppermute(pre, "head", [(i, (i + shift) % parts) for i in range(parts)]))
         for shift in range(1, parts)
     ]
     place = lax.axis_index("head").astype(jnp.int32).reshape(1)

time: 150 us -> 141 us (0.940)
  Pallas kernels: 19.9 us -> 8.46 us
  waiting for transfers between devices: 31.4 us -> 35.1 us
    pallas_call x7, Pallas kernels: 19.9 us -> 8.46 us  [call(): pl.pallas_call(kernel, out_shape=out_shape, in_specs=specs, name=kernel._...]
    all_to_all x2, waiting for transfers between devices: 29.1 us -> 33 us  [exchange(): return inside(lax.all_to_all(value, axis, 0, 0, tiled=True))]
  transfers between devices with their start and end apart: 5 -> 5, of which waited for: 3 -> 3; matrix products, arithmetic and copies ran while one was open for 0% -> 0% of each run, Pallas kernels for 3% -> 1%
where the time goes in v2:
time: 141 us; the launch traced here: 140 us
  blocking collectives  67.9 us (48%)
  waiting for transfers between devices  35.1 us (25%)
  starting transfers between devices  26.4 us (19%)
  Pallas kernels  8.46 us (6%)
  local copies, waits for them, and re-layouts  1.88 us (1%)
    all_to_all x2, blocking collectives, exchange(): return inside(lax.all_to_all(value, axis, 0, 0, tiled=True))  67.9 us
    all_to_all x2, waiting for transfers between devices, exchange(): return inside(lax.all_to_all(value, axis, 0, 0, tiled=True))  33 us
    all_to_all x2, starting transfers between devices, exchange(): return inside(lax.all_to_all(value, axis, 0, 0, tiled=True))  17.9 us
    pallas_call x7, Pallas kernels, call(): pl.pallas_call(kernel, out_shape=out_shape, in_specs=specs, name=kernel._...  8.46 us
    ppermute x3, starting transfers between devices, body(): lax.ppermute(pre, 'head', [(i, (i + shift) % parts) for i in range(parts)])  8.42 us
  transfers between devices with their start and end apart: 5, of which 3 were waited for; matrix products, arithmetic and copies ran while one was open for 0% of the time, Pallas kernels for 1%

profile of v2, /device:TPU:1, one launch (start us, length us, event | category | flops | bytes accessed | tf_op | source)
XLA Modules:
  0.0 140.5 jit_solution(18060141878735492441)
XLA Ops:
  0.6 0.9 copy-done.2
  1.5 0.9 copy-done.5
  2.5 0.1 pack_kernel.1
  2.6 0.0 copy-start
  2.6 0.0 copy-start.1
  2.6 0.0 copy-start.3
  2.6 0.0 copy-start.4
  2.6 0.0 copy-start.6
  2.6 17.1 %all_to_all.20.whole_ref = bf16[4,144,1024]{2,1,0:T(8,128)(2,1)S(1)} all-to-all(bf16[4,144,1024]{2,1,0:T(8,128)(2,1)S(1)} %pack_kernel.1), channel_id=1, replica_groups=mesh['seq'=32,'head'=4,'dp'=4] {'head'}, dimensions={0} | all-to-all | bytes 2359296 | tf_op jit(solution)/shard_map/all_to_all | solution.py:280
  19.7 2.1 %state_kernel.1 = (bf16[32,72,128]{2,1,0:T(8,128)(2,1)S(1)}, f32[3,16,128]{2,1,0:T(8,128)S(1)}, bf16[128,1024]{1,0:T(8,128)(2,1)S(1)}, bf16[128,1024]{1,0:T(8,128)(2,1)S(1)}) custom-call(bf16[4,144,1024]{2,1,0:T(8,128)(2,1)S(1)} %all_to_all.20.whole_ref, bf16[16,4096]{1,0:T(8,128)(2,1)S(1)} %bitcast.21, f32[1,16]{1,0:T(1,128)S(1)} %bitcast.31, ...), custom_call_target="tpu_custom_call" | custom-call | bytes 6000000 | tf_op jit(solution)/shard_map/state_kernel/pallas_call | solution.py:273
  21.8 50.9 %all_to_all.21.states_ref = bf16[32,72,128]{2,1,0:T(8,128)(2,1)S(1)} all-to-all(bf16[32,72,128]{2,1,0:T(8,128)(2,1)S(1)} %get-tuple-element.17), channel_id=1, replica_groups=mesh['seq'=32,'head'=4,'dp'=4] {'seq'}, dimensions={0} | all-to-all | bytes 1179648 | tf_op jit(solution)/shard_map/all_to_all | solution.py:280
  72.7 0.9 scan_kernel.1
  73.6 7.4 %all-to-all-start.2 = ((bf16[32,64,128]{2,1,0:T(8,128)(2,1)}), bf16[32,64,128]{2,1,0:T(8,128)(2,1)S(1)}, u32[]{:S(2)}, u32[]{:S(2)}) async-start(bf16[32,64,128]{2,1,0:T(8,128)(2,1)} %scan_kernel.1), calls=%async_computation.2 | async-start | bytes 1048576 | tf_op jit(solution)/shard_map/all_to_all | solution.py:280
  81.0 1.1 inner_kernel.1
  82.1 28.8 %all-to-all-done.2.states_ref = bf16[32,64,128]{2,1,0:T(8,128)(2,1)S(1)} async-done(((bf16[32,64,128]{2,1,0:T(8,128)(2,1)}), bf16[32,64,128]{2,1,0:T(8,128)(2,1)S(1)}, u32[]{:S(2)}, u32[]{:S(2)}) %all-to-all-start.2) | async-done | bytes 524320 | tf_op jit(solution)/shard_map/all_to_all | solution.py:280
  110.9 2.5 %last_kernel.1 = (bf16[128,1024]{1,0:T(8,128)(2,1)}, bf16[128,128]{1,0:T(8,128)(2,1)}, bf16[128,128]{1,0:T(8,128)(2,1)}, bf16[16,128]{1,0:T(8,128)(2,1)S(1)}, bf16[128,4,128]{2,1,0:T(4,128)(2,1)}) custom-call(bf16[32,64,128]{2,1,0:T(8,128)(2,1)S(1)} %all-to-all-done.2.states_ref, f32[3,16,128]{2,1,0:T(8,128)S(1)} %get-tuple-element.18.small_ref, ...), custom_call_target="tpu_custom_call" | custom-call | bytes 6000000 | tf_op jit(solution)/shard_map/last_kernel/pallas_call | solution.py:273
  113.4 10.6 %all-to-all-start.3 = ((bf16[128,4,128]{2,1,0:T(4,128)(2,1)}), bf16[128,4,128]{2,1,0:T(4,128)(2,1)S(1)}, u32[]{:S(2)}, u32[]{:S(2)}) async-start(bf16[128,4,128]{2,1,0:T(4,128)(2,1)} %get-tuple-element.28), calls=%async_computation.3 | async-start | bytes 262144 | tf_op jit(solution)/shard_map/all_to_all | solution.py:280
  124.0 2.2 %collective-permute-start = (bf16[16,128]{1,0:T(8,128)(2,1)S(1)}, bf16[16,128]{1,0:T(8,128)(2,1)S(1)}, u32[]{:S(2)}, u32[]{:S(2)}) collective-permute-start(bf16[16,128]{1,0:T(8,128)(2,1)S(1)} %get-tuple-element.27.refs_0_), channel_id=1, source_target_pairs={{0,4},{4,8},{8,12},{12,0},{1,5},{5,9},{9,13},{13,1},{2,6},{6,10},{... | collective-permute-start | bytes 12296 | tf_op jit(solution)/shard_map/ppermute | solution.py:333
  126.2 3.7 %collective-permute-start.1 = (bf16[16,128]{1,0:T(8,128)(2,1)S(1)}, bf16[16,128]{1,0:T(8,128)(2,1)S(1)}, u32[]{:S(2)}, u32[]{:S(2)}) collective-permute-start(bf16[16,128]{1,0:T(8,128)(2,1)S(1)} %get-tuple-element.27.refs_0_), channel_id=1, source_target_pairs={{0,8},{4,12},{8,0},{12,4},{1,9},{5,13},{9,1},{13,5},{2,10},{6,14},... | collective-permute-start | bytes 12296 | tf_op jit(solution)/shard_map/ppermute | solution.py:333
  129.9 2.5 %collective-permute-start.2 = (bf16[16,128]{1,0:T(8,128)(2,1)S(1)}, bf16[16,128]{1,0:T(8,128)(2,1)S(1)}, u32[]{:S(2)}, u32[]{:S(2)}) collective-permute-start(bf16[16,128]{1,0:T(8,128)(2,1)S(1)} %get-tuple-element.27.refs_0_), channel_id=1, source_target_pairs={{0,12},{4,0},{8,4},{12,8},{1,13},{5,1},{9,5},{13,9},{2,14},{6,2},{... | collective-permute-start | bytes 12296 | tf_op jit(solution)/shard_map/ppermute | solution.py:333
  132.4 2.1 %collective-permute-done.2.refs_3_ = bf16[16,128]{1,0:T(8,128)(2,1)S(1)} collective-permute-done((bf16[16,128]{1,0:T(8,128)(2,1)S(1)}, bf16[16,128]{1,0:T(8,128)(2,1)S(1)}, u32[]{:S(2)}, u32[]{:S(2)}) %collective-permute-start.2) | collective-permute-done | bytes 4128 | tf_op jit(solution)/shard_map/ppermute | solution.py:333
  134.5 1.0 input_kernel.1
  135.5 4.2 %all-to-all-done.3.part_ref = bf16[128,4,128]{2,1,0:T(4,128)(2,1)S(1)} async-done(((bf16[128,4,128]{2,1,0:T(4,128)(2,1)}), bf16[128,4,128]{2,1,0:T(4,128)(2,1)S(1)}, u32[]{:S(2)}, u32[]{:S(2)}) %all-to-all-start.3) | async-done | bytes 131104 | tf_op jit(solution)/shard_map/all_to_all | solution.py:280
  139.7 0.8 sum_kernel.1
  (11 shorter events, 0.0 us)
Async XLA Ops:
  0.6 0.9 copy-start.2
  1.5 0.9 copy-start.5
  2.6 17.1 %copy-start = (bf16[1,128,1024]{2,1,0:T(8,128)(2,1)S(1)}, bf16[1,128,1024]{2,1,0:T(8,128)(2,1)}, u32[]{:S(2)}) copy-start(bf16[1,128,1024]{2,1,0:T(8,128)(2,1)} %param.9) | copy-start | bytes 786436
  2.6 17.1 %copy-start.1 = (bf16[1,128,1024]{2,1,0:T(8,128)(2,1)S(1)}, bf16[1,128,1024]{2,1,0:T(8,128)(2,1)}, u32[]{:S(2)}) copy-start(bf16[1,128,1024]{2,1,0:T(8,128)(2,1)} %param.12) | copy-start | bytes 786436
  2.6 17.1 %copy-start.3 = (bf16[1,128,128]{2,1,0:T(8,128)(2,1)S(1)}, bf16[1,128,128]{2,1,0:T(8,128)(2,1)}, u32[]{:S(2)}) copy-start(bf16[1,128,128]{2,1,0:T(8,128)(2,1)} %param.10) | copy-start | bytes 98308
  2.6 17.1 %copy-start.4 = (bf16[1,128,128]{2,1,0:T(8,128)(2,1)S(1)}, bf16[1,128,128]{2,1,0:T(8,128)(2,1)}, u32[]{:S(2)}) copy-start(bf16[1,128,128]{2,1,0:T(8,128)(2,1)} %param.11) | copy-start | bytes 98308
  2.6 17.1 %copy-start.6 = (f32[16]{0:T(128)S(1)}, f32[16]{0:T(128)}, u32[]{:S(2)}) copy-start(f32[16]{0:T(128)} %param.15) | copy-start | bytes 196
  2.6 17.1 %copy-start.7 = (f32[16]{0:T(128)S(1)}, f32[16]{0:T(128)}, u32[]{:S(2)}) copy-start(f32[16]{0:T(128)} %param.14) | copy-start | bytes 196
  73.6 37.3 %all-to-all-start.2 = ((bf16[32,64,128]{2,1,0:T(8,128)(2,1)}), bf16[32,64,128]{2,1,0:T(8,128)(2,1)S(1)}, u32[]{:S(2)}, u32[]{:S(2)}) async-start(bf16[32,64,128]{2,1,0:T(8,128)(2,1)} %scan_kernel.1), calls=%async_computation.2 | async-start | bytes 1048576 | tf_op jit(solution)/shard_map/all_to_all | solution.py:280
  113.4 26.3 %all-to-all-start.3 = ((bf16[128,4,128]{2,1,0:T(4,128)(2,1)}), bf16[128,4,128]{2,1,0:T(4,128)(2,1)S(1)}, u32[]{:S(2)}, u32[]{:S(2)}) async-start(bf16[128,4,128]{2,1,0:T(4,128)(2,1)} %get-tuple-element.28), calls=%async_computation.3 | async-start | bytes 262144 | tf_op jit(solution)/shard_map/all_to_all | solution.py:280
  124.0 8.5 %collective-permute-start = (bf16[16,128]{1,0:T(8,128)(2,1)S(1)}, bf16[16,128]{1,0:T(8,128)(2,1)S(1)}, u32[]{:S(2)}, u32[]{:S(2)}) collective-permute-start(bf16[16,128]{1,0:T(8,128)(2,1)S(1)} %get-tuple-element.27.refs_0_), channel_id=1, source_target_pairs={{0,4},{4,8},{8,12},{12,0},{1,5},{5,9},{9,13},{13,1},{2,6},{6,10},{... | collective-permute-start | bytes 12296 | tf_op jit(solution)/shard_map/ppermute | solution.py:333
  126.2 6.3 %collective-permute-start.1 = (bf16[16,128]{1,0:T(8,128)(2,1)S(1)}, bf16[16,128]{1,0:T(8,128)(2,1)S(1)}, u32[]{:S(2)}, u32[]{:S(2)}) collective-permute-start(bf16[16,128]{1,0:T(8,128)(2,1)S(1)} %get-tuple-element.27.refs_0_), channel_id=1, source_target_pairs={{0,8},{4,12},{8,0},{12,4},{1,9},{5,13},{9,1},{13,5},{2,10},{6,14},... | collective-permute-start | bytes 12296 | tf_op jit(solution)/shard_map/ppermute | solution.py:333
  129.9 4.6 %collective-permute-start.2 = (bf16[16,128]{1,0:T(8,128)(2,1)S(1)}, bf16[16,128]{1,0:T(8,128)(2,1)S(1)}, u32[]{:S(2)}, u32[]{:S(2)}) collective-permute-start(bf16[16,128]{1,0:T(8,128)(2,1)S(1)} %get-tuple-element.27.refs_0_), channel_id=1, source_target_pairs={{0,12},{4,0},{8,4},{12,8},{1,13},{5,1},{9,5},{13,9},{2,14},{6,2},{... | collective-permute-start | bytes 12296 | tf_op jit(solution)/shard_map/ppermute | solution.py:333

commit v3 on v2

v3 whole, which is shorter than its diff:
```python
import jax
import jax.numpy as jnp
from jax import lax
from jax.experimental import pallas as pl
from jax.experimental.pallas import tpu as pltpu
from jax.sharding import PartitionSpec as P


P_SIZE = 64
NSTATE = 128
LANES = 128
NEAR = 4
EXTRA = 16
F32 = jnp.float32
BF16 = jnp.bfloat16
EXACT = lax.Precision.HIGHEST


def dot(a, b, ca, cb, precision=None):
    return lax.dot_general(
        a, b, (((ca,), (cb,)), ((), ())), preferred_element_type=F32, precision=precision
    )


def iota(shape, axis):
    return lax.broadcasted_iota(jnp.int32, shape, axis)


def halves(value):
    high = value.astype(BF16)
    return high, (value - high.astype(F32)).astype(BF16)


def thirds(value):
    first = value.astype(BF16).astype(F32)
    second = (value - first).astype(BF16).astype(F32)
    return first, second, value - first - second


def segment_matrix(rows, each, at):
    shape = (rows, each * P_SIZE)
    head = iota(shape, 0) - at * each
    lane = iota(shape, 1)
    inside = jnp.logical_and(lane >= head * P_SIZE, lane < head * P_SIZE + P_SIZE)
    return jnp.where(inside, 1.0, 0.0).astype(BF16)


def column(row, place, rows, each):
    size = row.shape[1]
    shape = (rows, size)
    mine = iota(shape, 1) == place * each + lax.rem(iota(shape, 0), each)
    return jnp.sum(jnp.where(mine, row, 0.0), axis=1, keepdims=True)


def spread(parts, segments):
    return dot(parts[0], segments, 1, 0) + dot(parts[1], segments, 1, 0)


def gathered(value, segments):
    high, low = halves(value)
    return dot(segments, high, 1, 1) + dot(segments, low, 1, 1)


def views(data_ref, at, wide):
    return (
        data_ref[at, :, :wide],
        data_ref[at, :, wide : 2 * wide],
        data_ref[at, :, 2 * wide : 2 * wide + NSTATE],
        data_ref[at, :, 2 * wide + NSTATE :],
    )


def pack_kernel(input_ref, weight_ref, out_ref):
    parts, _, width = out_ref.shape
    tokens = input_ref.shape[0]
    for part in range(parts):
        out_ref[part, :tokens, :] = input_ref[...]
        out_ref[part, tokens:, :] = weight_ref[:, part * width : (part + 1) * width]


def data_kernel(x_ref, g_ref, b_ref, c_ref, *out_refs):
    wide = x_ref.shape[1] // NEAR

    def fill(out_ref, quarter):
        lanes = slice(quarter * wide, (quarter + 1) * wide)
        out_ref[:, :wide] = x_ref[:, lanes]
        out_ref[:, wide : 2 * wide] = g_ref[:, lanes]

    for shift, out_ref in enumerate(out_refs):
        target = lax.rem(lax.rem(lax.axis_index("seq"), NEAR) + shift, NEAR)
        for quarter in range(NEAR):
            pl.when(target == quarter)(lambda o=out_ref, q=quarter: fill(o, q))
        out_ref[:, 2 * wide : 2 * wide + NSTATE] = b_ref[...]
        out_ref[:, 2 * wide + NSTATE :] = c_ref[...]


def preact_kernel(whole_ref, weight_ref, bias_ref, out_ref):
    parts, _, width = whole_ref.shape
    near, each, tokens = out_ref.shape
    term = column(bias_ref[...], 0, near * each, near * each)
    for part in range(parts):
        term = term + dot(
            weight_ref[:, part * width : (part + 1) * width], whole_ref[part, :tokens, :], 1, 1
        )
    out_ref[...] = term.reshape(near, each, tokens)


def state_kernel(terms_ref, log_ref, *refs):
    received = refs[:NEAR]
    sent_ref, data_ref, small_ref, states_ref, scaled_ref = refs[NEAR:]
    each, tokens = terms_ref.shape[1:]
    rows = NEAR * each
    wide = each * P_SIZE
    place = lax.rem(lax.axis_index("seq"), NEAR)
    for shift in range(NEAR):
        data_ref[lax.rem(place + NEAR - shift, NEAR)] = received[shift][...]
    preact = jnp.concatenate([terms_ref[at] for at in range(NEAR)], axis=0)
    tail = jnp.exp(-jnp.abs(preact))
    step = jnp.maximum(preact, 0.0) + jnp.log1p(tail)
    rate = jnp.exp(column(log_ref[...], place, rows, each))
    upto = jnp.where(iota((tokens, tokens), 0) <= iota((tokens, tokens), 1), 1.0, 0.0)
    cumulated = dot(-rate * step, upto, 1, 0, EXACT)
    total = cumulated[:, tokens - 1 :]
    small_ref[0] = preact
    small_ref[1] = step
    small_ref[2] = cumulated
    small_ref[3] = jnp.broadcast_to(rate, cumulated.shape)
    inflow = halves(jnp.transpose(jnp.exp(total - cumulated) * step))
    since = halves(jnp.transpose(jnp.exp(cumulated)))
    for at in range(NEAR):
        segments = segment_matrix(rows, each, at)
        x, g, b, c = views(data_ref, at, wide)
        scaled = (x.astype(F32) * spread(inflow, segments)).astype(BF16)
        scaled_ref[0, at] = scaled
        states_ref[0, at] = dot(scaled, b, 0, 0).astype(BF16)
        scaled = (g.astype(F32) * spread(since, segments)).astype(BF16)
        scaled_ref[1, at] = scaled
        states_ref[1, at] = dot(scaled, c, 0, 0).astype(BF16)
    shrink = jnp.exp(total)
    slices = sent_ref.shape[0]
    piece = wide // slices
    line = iota((EXTRA, NSTATE), 0)
    for head in range(each):
        lines = slice(head * P_SIZE, (head + 1) * P_SIZE)
        factor = [shrink[at * each + head : at * each + head + 1] for at in range(NEAR)]
        both = []
        for which, order in ((0, range(NEAR)), (1, reversed(range(NEAR)))):
            state = None
            for at in order:
                here = states_ref[which, at, lines, :].astype(F32)
                state = here if state is None else factor[at] * state + here
            both.append(state)
        whole = factor[0]
        for at in range(1, NEAR):
            whole = whole * factor[at]
        first, second, third = thirds(whole)
        tile = jnp.where(line == 0, first, jnp.where(line == 1, second, third))
        tile = jnp.where(line < 3, tile, 0.0).astype(BF16)
        for part in range(P_SIZE // piece):
            index = head * (P_SIZE // piece) + part
            for which in range(2):
                sent_ref[index, which * piece : (which + 1) * piece, :] = both[which][
                    part * piece : (part + 1) * piece
                ].astype(BF16)
            sent_ref[index, 2 * piece :, :] = tile


def far_kernel(states_ref, out_ref):
    count, rows2, _ = out_ref.shape
    rows = rows2 // 2
    shrink = [
        jnp.sum(states_ref[at, rows2 : rows2 + 3, :].astype(F32), axis=0, keepdims=True)
        for at in range(count)
    ]
    for start, order in ((0, range(count)), (rows, reversed(range(count)))):
        state = jnp.zeros((rows, NSTATE), F32)
        for at in order:
            out_ref[at, start : start + rows, :] = state.astype(BF16)
            state = shrink[at] * state + states_ref[at, start : start + rows, :].astype(F32)


def inner_kernel(data_ref, small_ref, inner_ref, pair_ref, sums_ref):
    _, rows, tokens = small_ref.shape
    each = rows // NEAR
    wide = each * P_SIZE
    cumulated = small_ref[2]
    step_column = jnp.transpose(small_ref[1])
    cumulated_column = jnp.transpose(cumulated)
    allowed = iota((tokens, tokens), 0) <= iota((tokens, tokens), 1)
    lower = iota((tokens, LANES), 1) < P_SIZE
    zero = jnp.zeros((tokens, LANES), BF16)
    row_sums = []
    direct = jnp.zeros((rows, tokens), F32)
    for at in range(NEAR):
        x_all, g_all, b, c = views(data_ref, at, wide)
        kernel = dot(b, c, 1, 1)
        d_kernel = jnp.zeros((tokens, tokens), F32)
        products = []
        for pair in range(each // 2):
            lanes = slice(pair * LANES, (pair + 1) * LANES)
            x = x_all[:, lanes]
            g = g_all[:, lanes]
            both = []
            for half in range(2):
                row = at * each + 2 * pair + half
                span = cumulated[row : row + 1, :] - cumulated_column[:, row : row + 1]
                span = jnp.exp(jnp.where(allowed, span, -1e30))
                mine = jnp.where(lower, x, zero) if half == 0 else jnp.where(lower, zero, x)
                product = dot(mine, g, 1, 1) * span * step_column[:, row : row + 1]
                d_kernel = d_kernel + product
                row_sums.append(jnp.sum(product * kernel, axis=0, keepdims=True))
                both.append(dot((span * kernel).astype(BF16), g, 1, 0))
            inner = jnp.where(lower, both[0], both[1])
            inner_ref[at, :, lanes] = inner.astype(BF16)
            products.append(x.astype(F32) * inner)
        d_kernel = d_kernel.astype(BF16)
        pair_ref[0, at] = dot(d_kernel, c, 1, 0).astype(BF16)
        pair_ref[1, at] = dot(d_kernel, b, 0, 0).astype(BF16)
        direct = direct + gathered(
            jnp.concatenate(products, axis=1), segment_matrix(rows, each, at)
        )
    sums_ref[0] = jnp.concatenate(row_sums, axis=0)
    sums_ref[1] = direct


def last_kernel(
    far_ref, data_ref, small_ref, states_ref, scaled_ref, inner_ref, pair_ref,
    sums_ref, *refs
):
    own_refs = refs[:NEAR]
    pre_ref, result_ref = refs[NEAR:]
    _, rows, tokens = small_ref.shape
    each = rows // NEAR
    wide = each * P_SIZE
    place = lax.rem(lax.axis_index("seq"), NEAR)
    preact = small_ref[0]
    step = small_ref[1]
    cumulated = small_ref[2]
    total = cumulated[:, tokens - 1 :]
    shrink = jnp.exp(total)
    rate = small_ref[3]
    left = jnp.exp(total - cumulated)
    piece = far_ref.shape[1] // 2

    def faded(state, at):
        return jnp.concatenate(
            [
                shrink[at * each + head : at * each + head + 1]
                * state[head * P_SIZE : (head + 1) * P_SIZE]
                for head in range(each)
            ],
            axis=0,
        )

    coming = [far_ref[:, :piece, :].reshape(wide, NSTATE).astype(F32)]
    for at in range(NEAR - 1):
        coming.append(faded(coming[at], at) + states_ref[0, at].astype(F32))
    leaving = [far_ref[:, piece:, :].reshape(wide, NSTATE).astype(F32)]
    for at in reversed(range(1, NEAR)):
        leaving.insert(0, faded(leaving[0], at) + states_ref[1, at].astype(F32))
    step_halves = halves(jnp.transpose(step))
    left_halves = halves(jnp.transpose(left))
    from_inflow = jnp.zeros((rows, tokens), F32)
    from_readout = jnp.zeros((rows, tokens), F32)
    meeting = jnp.zeros((rows, NSTATE), F32)
    for at in range(NEAR):
        segments = segment_matrix(rows, each, at)
        x, g, b, c = views(data_ref, at, wide)
        state = coming[at].astype(BF16)
        grad = leaving[at].astype(BF16)
        from_grad = dot(b, grad, 1, 1)
        from_state = dot(c, state, 1, 1)
        result_ref[at, :, :wide] = (
            spread(step_halves, segments)
            * (inner_ref[at].astype(F32) + spread(left_halves, segments) * from_grad)
        ).astype(BF16)
        result_ref[at, :, wide : wide + NSTATE] = (
            pair_ref[0, at].astype(F32) + dot(scaled_ref[0, at], grad, 1, 0)
        ).astype(BF16)
        result_ref[at, :, wide + NSTATE :] = (
            pair_ref[1, at].astype(F32) + dot(scaled_ref[1, at], state, 1, 0)
        ).astype(BF16)
        from_inflow = from_inflow + gathered(x.astype(F32) * from_grad, segments)
        from_readout = from_readout + gathered(g.astype(F32) * from_state, segments)
        high, low = halves(coming[at] * leaving[at])
        meeting = meeting + dot(segments, high, 1, 0) + dot(segments, low, 1, 0)
    inflow_part = left * from_inflow
    direct = sums_ref[1] + inflow_part
    of_total = jnp.sum(step * inflow_part, axis=1, keepdims=True) + shrink * jnp.sum(
        meeting, axis=1, keepdims=True
    )
    of_cumulated = sums_ref[0] + jnp.exp(cumulated) * from_readout - step * direct
    onward = jnp.where(iota((tokens, tokens), 0) >= iota((tokens, tokens), 1), 1.0, 0.0)
    of_decay = dot(of_cumulated, onward, 1, 0, EXACT) + of_total
    grad_step = direct - rate * of_decay
    sigmoid = 1.0 / (1.0 + jnp.exp(-preact))
    grad_pre = grad_step * sigmoid
    parts = pre_ref.shape[0] // NEAR
    for at in range(NEAR):
        rounded = grad_pre[at * each : (at + 1) * each].astype(BF16)
        for part in range(parts):
            pre_ref[at * parts + part] = rounded
    for shift in range(NEAR):
        own_refs[shift][...] = result_ref[lax.rem(place + shift, NEAR)]


def part_kernel(pre_ref, whole_ref, part_ref):
    parts, _, width = whole_ref.shape
    tokens = pre_ref.shape[2]
    each = pre_ref.shape[1]
    heads = NEAR * each
    group_place = lax.axis_index("head")
    grad_pre = jnp.concatenate(
        [pre_ref[near * parts + group_place].astype(F32) for near in range(NEAR)], axis=0
    ).astype(BF16)
    per = part_ref.shape[1]
    shards = heads // per
    size = LANES // shards
    shape = (heads, heads)
    swapped = iota(shape, 1) == shards * lax.rem(iota(shape, 0), per) + iota(shape, 0) // per
    swapped = dot(jnp.where(swapped, 1.0, 0.0).astype(BF16), grad_pre, 1, 0).astype(BF16)
    group = 8 // per
    block = iota((8, LANES), 1) // size
    row = iota((8, LANES), 0) // per
    masks = [
        jnp.logical_and(block == index, row == index % group) for index in range(shards)
    ]
    for source in range(parts):
        term = dot(swapped, whole_ref[source, :tokens, :], 1, 0)
        for index in range(width // LANES):
            lanes = slice(index * LANES, (index + 1) * LANES)
            turned = []
            for first in range(0, heads, 8):
                piece = term[first : first + 8, lanes]
                turned.append(
                    [piece] + [pltpu.roll(piece, size * turn, 1) for turn in range(1, shards)]
                )
            for shard in range(shards):
                packed = jnp.zeros((8, LANES), F32)
                for index2 in range(shards):
                    chosen = turned[index2 // group][(index2 - shard) % shards]
                    packed = jnp.where(masks[index2], chosen, packed)
                total_rows = packed[:per]
                for other in range(1, group):
                    total_rows = total_rows + packed[other * per : (other + 1) * per]
                where = (source * (width // LANES) + index) * shards + shard
                part_ref[where] = total_rows.astype(part_ref.dtype)


def input_kernel(pre_ref, whole_ref, out_ref):
    parts, _, width = whole_ref.shape
    tokens = pre_ref.shape[2]
    weights = whole_ref[:, tokens:, :]
    heads = weights.shape[1]
    pre = jnp.concatenate(
        [
            pre_ref[near * parts + part].astype(F32)
            for part in range(parts)
            for near in range(NEAR)
        ],
        axis=0,
    ).astype(BF16)
    out_ref[...] = dot(pre, weights.reshape(parts * heads, width), 0, 0).astype(BF16)


def final_kernel(*refs):
    received = refs[:NEAR]
    gx_ref, gb_ref, gc_ref = refs[NEAR:]
    wide = gx_ref.shape[1] // NEAR

    def fill(ref, quarter):
        gx_ref[:, quarter * wide : (quarter + 1) * wide] = ref[:, :wide]

    for shift, ref in enumerate(received):
        source = lax.rem(lax.rem(lax.axis_index("seq"), NEAR) + NEAR - shift, NEAR)
        for quarter in range(NEAR):
            pl.when(source == quarter)(lambda r=ref, q=quarter: fill(r, q))
    for out_ref, first in ((gb_ref, wide), (gc_ref, wide + NSTATE)):
        total = received[0][:, first : first + NSTATE].astype(F32)
        for ref in received[1:]:
            total = total + ref[:, first : first + NSTATE].astype(F32)
        out_ref[...] = total.astype(BF16)


def sum_kernel(part_ref, out_ref):
    heads, size = out_ref.shape
    total = jnp.sum(part_ref[...].astype(F32), axis=0)
    per = total.shape[0]
    shards = heads // per
    for shard in range(shards):
        piece = total[:, shard * size : (shard + 1) * size]
        for row in range(per):
            head = row * shards + shard
            out_ref[head : head + 1, :] = piece[row : row + 1, :]


def inside(value):
    return pltpu.with_memory_space_constraint(value, pltpu.VMEM)


def call(kernel, out_shape, *args, scratch=()):
    cost = pl.CostEstimate(flops=0, transcendentals=0, bytes_accessed=4_000_000)
    specs = [pl.BlockSpec(memory_space=pltpu.VMEM)] * len(args)
    return pl.pallas_call(
        kernel, out_shape=out_shape, in_specs=specs, scratch_shapes=scratch,
        cost_estimate=cost,
        compiler_params=pltpu.CompilerParams(vmem_limit_bytes=32 * 2**20),
    )(*args)


def outside(value):
    return pltpu.with_memory_space_constraint(value, pltpu.HBM)


def exchange(value, axis, groups=None):
    return inside(lax.all_to_all(value, axis, 0, 0, tiled=True, axis_index_groups=groups))


def body(
    layer_input, head_input, in_matrix, out_matrix, grad_output, step_weight, step_bias, decay_log
):
    parts = lax.axis_size("head")
    places = lax.axis_size("seq")
    shards = lax.axis_size("dp")
    tokens, width = layer_input.shape[1:]
    heads = step_weight.shape[1]
    runs = places // NEAR
    each = heads // NEAR
    rows = NEAR * each
    wide = each * P_SIZE
    count = NEAR * parts
    near = [[run * NEAR + at for at in range(NEAR)] for run in range(runs)]
    far = [[run * NEAR + at for run in range(runs)] for at in range(NEAR)]
    block = [[run * count + index for index in range(count)] for run in range(runs)]
    shape = pltpu.HBM
    local = pltpu.VMEM

    def turn(value, shift):
        pairs = [
            (run * NEAR + at, run * NEAR + (at + shift) % NEAR)
            for run in range(runs)
            for at in range(NEAR)
        ]
        return outside(lax.ppermute(value, "seq", pairs))

    x, b, c, g = head_input[0], in_matrix[0], out_matrix[0], grad_output[0]
    bias = step_bias.reshape(1, heads)
    logs = decay_log.reshape(1, heads)
    weight = step_weight.T
    packed = call(
        pack_kernel, shape((parts, tokens + heads, width), BF16), layer_input[0], weight
    )
    whole = lax.all_to_all(packed, "head", 0, 0, tiled=True)
    kept = outside(whole)
    data = call(
        data_kernel,
        (shape((tokens, 2 * wide + 2 * NSTATE), BF16),) * NEAR,
        x, g, b, c,
    )
    received = [data[0]] + [turn(data[shift], shift) for shift in range(1, NEAR)]
    terms = call(preact_kernel, local((NEAR, each, tokens), F32), whole, weight, bias)
    terms = exchange(terms, "seq", near)
    sent, data, small, states, scaled = call(
        state_kernel,
        (
            local((runs, 2 * wide // runs + EXTRA, NSTATE), BF16),
            local((NEAR, tokens, 2 * wide + 2 * NSTATE), BF16),
            local((4, rows, tokens), F32),
            local((2, NEAR, wide, NSTATE), BF16),
            local((2, NEAR, tokens, wide), BF16),
        ),
        terms, logs, *received,
    )
    sent = exchange(sent, "seq", far)
    inner, pair, sums = call(
        inner_kernel,
        (
            local((NEAR, tokens, wide), BF16),
            local((2, NEAR, tokens, NSTATE), BF16),
            local((2, rows, tokens), F32),
        ),
        data, small,
    )
    back = call(far_kernel, local((runs, 2 * wide // runs, NSTATE), BF16), sent)
    back = exchange(back, "seq", far)
    *owned, pre = call(
        last_kernel,
        (shape((tokens, wide + 2 * NSTATE), BF16),) * NEAR + (local((count, each, tokens), BF16),),
        back, data, small, states, scaled, inner, pair, sums,
        scratch=(pltpu.VMEM((NEAR, tokens, wide + 2 * NSTATE), BF16),),
    )
    pre = exchange(pre, ("seq", "head"), block)
    part = call(
        part_kernel,
        local((places * shards, heads // shards, LANES), BF16),
        pre, kept,
    )
    part = exchange(part, ("seq", "dp"))
    returned = [owned[0]]
    for shift in range(1, NEAR):
        returned.append(turn(owned[shift], shift))
    grad_input = call(input_kernel, shape((tokens, width), BF16), pre, kept)
    grad_x, grad_b, grad_c = call(
        final_kernel,
        (shape(x.shape, BF16), shape(b.shape, BF16), shape(c.shape, BF16)),
        *returned,
    )
    term = call(sum_kernel, shape((heads, LANES // shards), F32), part)
    return (grad_x[None], grad_b[None], grad_c[None], grad_input[None], term.T)


def solution(mesh):
    in_specs = (P("dp", "seq", "head"),) * 5 + (P(None, "head"), P("head"), P("head"))
    out_specs = (P("dp", "seq", "head"),) * 4 + (P(("seq", "dp"), "head"),)
    return jax.shard_map(body, mesh=mesh, in_specs=in_specs, out_specs=out_specs, check_vma=False)
```

time: 141 us -> 137 us (0.972)
  blocking collectives: 67.9 us -> 41.9 us
  starting transfers between devices: 26.4 us -> 50.6 us
  waiting for transfers between devices: 35.1 us -> 20.5 us
  Pallas kernels: 8.46 us -> 18.7 us
    all_to_all x2, blocking collectives: 67.9 us -> 41.9 us  [exchange(): lax.all_to_all(value, axis, 0, 0, tiled=True, axis_index_groups=groups)]
    all_to_all x2 -> x4, waiting for transfers between devices: 33 us -> 14 us  [the longest x3 14 us: exchange(): lax.all_to_all(value, axis, 0, 0, tiled=True, axis_index_groups=groups)]
    ppermute x3 -> x6, starting transfers between devices: 8.42 us -> 21.5 us  [turn(): return outside(lax.ppermute(value, 'seq', pairs))]
    all_to_all x2 -> x4, starting transfers between devices: 17.9 us -> 29 us  [the longest x3 23.9 us: exchange(): lax.all_to_all(value, axis, 0, 0, tiled=True, axis_index_groups=groups)]
    pallas_call x7 -> x11, Pallas kernels: 8.46 us -> 18.7 us  [call(): pl.pallas_call(kernel, out_shape=out_shape, in_specs=specs, scratch_shape...]
    ppermute x3 -> x6, waiting for transfers between devices: 2.09 us -> 6.53 us  [turn(): return outside(lax.ppermute(value, 'seq', pairs))]
  transfers between devices with their start and end apart: 5 -> 10, of which waited for: 3 -> 4; matrix products, arithmetic and copies ran while one was open for 0% -> 0% of each run, Pallas kernels for 1% -> 6%
where the time goes in v3:
time: 137 us; the launch traced here: 135 us
  starting transfers between devices  50.6 us (37%)
  blocking collectives  41.9 us (31%)
  waiting for transfers between devices  20.5 us (15%)
  Pallas kernels  18.7 us (14%)
  local copies, waits for them, and re-layouts  2.62 us (2%)
    all_to_all x2, blocking collectives, exchange(): lax.all_to_all(value, axis, 0, 0, tiled=True, axis_index_groups=groups)  41.9 us
    all_to_all x3, starting transfers between devices, exchange(): lax.all_to_all(value, axis, 0, 0, tiled=True, axis_index_groups=groups)  23.9 us
    ppermute x6, starting transfers between devices, turn(): return outside(lax.ppermute(value, 'seq', pairs))  21.5 us
    pallas_call x11, Pallas kernels, call(): pl.pallas_call(kernel, out_shape=out_shape, in_specs=specs, scratch_shape...  18.7 us
    all_to_all x3, waiting for transfers between devices, exchange(): lax.all_to_all(value, axis, 0, 0, tiled=True, axis_index_groups=groups)  14 us
    ppermute x6, waiting for transfers between devices, turn(): return outside(lax.ppermute(value, 'seq', pairs))  6.53 us
    all_to_all x1, starting transfers between devices, body(): whole = lax.all_to_all(packed, 'head', 0, 0, tiled=True)  5.14 us
  transfers between devices with their start and end apart: 10, of which 4 were waited for; matrix products, arithmetic and copies ran while one was open for 0% of the time, Pallas kernels for 6%

profile of v3, /device:TPU:1, one launch (start us, length us, event | category | flops | bytes accessed | tf_op | source)
XLA Modules:
  0.0 135.1 jit_solution(4329661519701479484)
XLA Ops:
  2.5 1.1 shard_map.119
  3.6 5.1 %all-to-all-start = ((bf16[4,144,1024]{2,1,0:T(8,128)(2,1)}), bf16[4,144,1024]{2,1,0:T(8,128)(2,1)S(1)}, u32[]{:S(2)}, u32[]{:S(2)}) async-start(bf16[4,144,1024]{2,1,0:T(8,128)(2,1)} %shard_map.119), calls=%async_computation | async-start | bytes 2359296 | tf_op jit(solution)/shard_map/all_to_all | solution.py:453
  8.8 1.1 shard_map.121
  9.9 3.7 %collective-permute-start = (bf16[128,768]{1,0:T(8,128)(2,1)}, bf16[128,768]{1,0:T(8,128)(2,1)S(1)}, u32[]{:S(2)}, u32[]{:S(2)}) collective-permute-start(bf16[128,768]{1,0:T(8,128)(2,1)} %get-tuple-element.26), channel_id=1, source_target_pairs={{0,16},{16,32},{32,48},{48,0},{64,80},{80,96},{96,112},{112,64},{1... | collective-permute-start | bytes 589832 | tf_op jit(solution)/shard_map/ppermute | solution.py:444
  13.6 4.9 %collective-permute-start.1 = (bf16[128,768]{1,0:T(8,128)(2,1)}, bf16[128,768]{1,0:T(8,128)(2,1)S(1)}, u32[]{:S(2)}, u32[]{:S(2)}) collective-permute-start(bf16[128,768]{1,0:T(8,128)(2,1)} %get-tuple-element.27), channel_id=1, source_target_pairs={{0,32},{16,48},{32,0},{48,16},{64,96},{80,112},{96,64},{112,80},{1... | collective-permute-start | bytes 589832 | tf_op jit(solution)/shard_map/ppermute | solution.py:444
  18.5 2.6 %collective-permute-start.2 = (bf16[128,768]{1,0:T(8,128)(2,1)}, bf16[128,768]{1,0:T(8,128)(2,1)S(1)}, u32[]{:S(2)}, u32[]{:S(2)}) collective-permute-start(bf16[128,768]{1,0:T(8,128)(2,1)} %get-tuple-element.28), channel_id=1, source_target_pairs={{0,48},{16,0},{32,16},{48,32},{64,112},{80,64},{96,80},{112,96},{1... | collective-permute-start | bytes 589832 | tf_op jit(solution)/shard_map/ppermute | solution.py:444
  22.2 8.9 %all-to-all-start.1 = ((f32[4,4,128]{2,1,0:T(4,128)}), f32[4,4,128]{2,1,0:T(4,128)S(1)}, u32[]{:S(2)}, u32[]{:S(2)}) async-start(f32[4,4,128]{2,1,0:T(4,128)} %shard_map.120), calls=%async_computation.1 | async-start | bytes 16384 | tf_op jit(solution)/shard_map/all_to_all | solution.py:416
  31.1 1.3 collective-permute-done.2.refs_3_
  32.4 3.1 %all-to-all-done.1.terms_ref = f32[4,4,128]{2,1,0:T(4,128)S(1)} async-done(((f32[4,4,128]{2,1,0:T(4,128)}), f32[4,4,128]{2,1,0:T(4,128)S(1)}, u32[]{:S(2)}, u32[]{:S(2)}) %all-to-all-start.1) | async-done | bytes 8224 | tf_op jit(solution)/shard_map/all_to_all | solution.py:416
  35.5 3.5 %shard_map.122 = (bf16[8,80,128]{2,1,0:T(8,128)(2,1)S(1)}, bf16[4,128,768]{2,1,0:T(8,128)(2,1)S(1)}, f32[4,16,128]{2,1,0:T(8,128)S(1)}, bf16[2,4,256,128]{3,2,1,0:T(8,128)(2,1)S(1)}, bf16[2,4,128,256]{3,2,1,0:T(8,128)(2,1)S(1)}) custom-call(f32[4,4,128]{2,1,0:T(4,128)S(1)} %all-to-all-done.1.terms_ref, f32[1,16]{1,0:T(1,128)S(1)} %bitcast.21, ...), custom_call_target="tpu_custom_call" | custom-call | bytes 4000000 | tf_op jit(solution)/shard_map/pallas_call | solution.py:404
  39.1 26.1 %all_to_all.30.states_ref = bf16[8,80,128]{2,1,0:T(8,128)(2,1)S(1)} all-to-all(bf16[8,80,128]{2,1,0:T(8,128)(2,1)S(1)} %get-tuple-element.29), channel_id=1, replica_groups={{0,64,128,192,256,320,384,448},{16,80,144,208,272,336,400,464},{32,96,1..., dimensions={0} | all-to-all | bytes 327680 | tf_op jit(solution)/shard_map/all_to_all | solution.py:416
  65.9 4.3 %all-to-all-start.3 = ((bf16[8,64,128]{2,1,0:T(8,128)(2,1)}), bf16[8,64,128]{2,1,0:T(8,128)(2,1)S(1)}, u32[]{:S(2)}, u32[]{:S(2)}) async-start(bf16[8,64,128]{2,1,0:T(8,128)(2,1)} %shard_map.123), calls=%async_computation.3 | async-start | bytes 262144 | tf_op jit(solution)/shard_map/all_to_all | solution.py:416
  70.2 1.9 %shard_map.124 = (bf16[4,128,256]{2,1,0:T(8,128)(2,1)S(1)}, bf16[2,4,128,128]{3,2,1,0:T(8,128)(2,1)S(1)}, f32[2,16,128]{2,1,0:T(8,128)S(1)}) custom-call(bf16[4,128,768]{2,1,0:T(8,128)(2,1)S(1)} %get-tuple-element.30.data_ref, f32[4,16,128]{2,1,0:T(8,128)S(1)} %get-tuple-element.31.small_ref), custom_call_target="tpu_custom_call" | custom-call | bytes 4000000 | tf_op jit(solution)/shard_map/pallas_call | solution.py:404
  72.1 10.9 %all-to-all-done.3.far_ref = bf16[8,64,128]{2,1,0:T(8,128)(2,1)S(1)} async-done(((bf16[8,64,128]{2,1,0:T(8,128)(2,1)}), bf16[8,64,128]{2,1,0:T(8,128)(2,1)S(1)}, u32[]{:S(2)}, u32[]{:S(2)}) %all-to-all-start.3) | async-done | bytes 131104 | tf_op jit(solution)/shard_map/all_to_all | solution.py:416
  82.9 2.1 %shard_map.125 = (bf16[128,512]{1,0:T(8,128)(2,1)}, bf16[128,512]{1,0:T(8,128)(2,1)}, bf16[128,512]{1,0:T(8,128)(2,1)}, bf16[128,512]{1,0:T(8,128)(2,1)}, bf16[16,4,128]{2,1,0:T(4,128)(2,1)S(1)}) custom-call(bf16[8,64,128]{2,1,0:T(8,128)(2,1)S(1)} %all-to-all-done.3.far_ref, bf16[4,128,768]{2,1,0:T(8,128)(2,1)S(1)} %get-tuple-element.30.data_ref, ...), custom_call_target="tpu_custom_call" | custom-call | bytes 4000000 | tf_op jit(solution)/shard_map/pallas_call | solution.py:404
  85.1 15.8 %all_to_all.31.pre_ref = bf16[16,4,128]{2,1,0:T(4,128)(2,1)S(1)} all-to-all(bf16[16,4,128]{2,1,0:T(4,128)(2,1)S(1)} %get-tuple-element.44), channel_id=1, replica_groups={{0,4,8,12,16,20,24,28,32,36,40,44,48,52,56,60},{64,68,72,76,80,84,88,92..., dimensions={0} | all-to-all | bytes 32768 | tf_op jit(solution)/shard_map/all_to_all | solution.py:416
  100.9 2.4 %shard_map.128 = bf16[128,4,128]{2,1,0:T(4,128)(2,1)} custom-call(bf16[16,4,128]{2,1,0:T(4,128)(2,1)S(1)} %all_to_all.31.pre_ref, bf16[4,144,1024]{2,1,0:T(8,128)(2,1)} %copy-done), custom_call_target="tpu_custom_call" | custom-call | bytes 4000000 | tf_op jit(solution)/shard_map/pallas_call | solution.py:404
  103.3 10.7 %all-to-all-start.5 = ((bf16[128,4,128]{2,1,0:T(4,128)(2,1)}), bf16[128,4,128]{2,1,0:T(4,128)(2,1)S(1)}, u32[]{:S(2)}, u32[]{:S(2)}) async-start(bf16[128,4,128]{2,1,0:T(4,128)(2,1)} %shard_map.128), calls=%async_computation.5 | async-start | bytes 262144 | tf_op jit(solution)/shard_map/all_to_all | solution.py:416
  114.0 3.3 %collective-permute-start.3 = (bf16[128,512]{1,0:T(8,128)(2,1)S(1)}, bf16[128,512]{1,0:T(8,128)(2,1)S(1)}, u32[]{:S(2)}, u32[]{:S(2)}) collective-permute-start(bf16[128,512]{1,0:T(8,128)(2,1)S(1)} %copy-done.20), channel_id=1, source_target_pairs={{0,16},{16,32},{32,48},{48,0},{64,80},{80,96},{96,112},{112,64},{1... | collective-permute-start | bytes 393224 | tf_op jit(solution)/shard_map/ppermute | solution.py:444
  117.3 4.0 %collective-permute-start.4 = (bf16[128,512]{1,0:T(8,128)(2,1)S(1)}, bf16[128,512]{1,0:T(8,128)(2,1)S(1)}, u32[]{:S(2)}, u32[]{:S(2)}) collective-permute-start(bf16[128,512]{1,0:T(8,128)(2,1)S(1)} %copy-done.19), channel_id=1, source_target_pairs={{0,32},{16,48},{32,0},{48,16},{64,96},{80,112},{96,64},{112,80},{1... | collective-permute-start | bytes 393224 | tf_op jit(solution)/shard_map/ppermute | solution.py:444
  121.3 3.1 %collective-permute-start.5 = (bf16[128,512]{1,0:T(8,128)(2,1)S(1)}, bf16[128,512]{1,0:T(8,128)(2,1)S(1)}, u32[]{:S(2)}, u32[]{:S(2)}) collective-permute-start(bf16[128,512]{1,0:T(8,128)(2,1)S(1)} %copy-done.18), channel_id=1, source_target_pairs={{0,48},{16,0},{32,16},{48,32},{64,112},{80,64},{96,80},{112,96},{1... | collective-permute-start | bytes 393224 | tf_op jit(solution)/shard_map/ppermute | solution.py:444
  124.4 2.2 %shard_map.127 = bf16[128,1024]{1,0:T(8,128)(2,1)} custom-call(bf16[16,4,128]{2,1,0:T(4,128)(2,1)S(1)} %all_to_all.31.pre_ref, bf16[4,144,1024]{2,1,0:T(8,128)(2,1)} %copy-done), custom_call_target="tpu_custom_call" | custom-call | bytes 4000000 | tf_op jit(solution)/shard_map/pallas_call | solution.py:404
  126.6 5.2 %collective-permute-done.4.refs_2_ = bf16[128,512]{1,0:T(8,128)(2,1)S(1)} collective-permute-done((bf16[128,512]{1,0:T(8,128)(2,1)S(1)}, bf16[128,512]{1,0:T(8,128)(2,1)S(1)}, u32[]{:S(2)}, u32[]{:S(2)}) %collective-permute-start.4) | collective-permute-done | bytes 131104 | tf_op jit(solution)/shard_map/ppermute | solution.py:444
  132.5 1.8 %shard_map.126 = (bf16[128,1024]{1,0:T(8,128)(2,1)}, bf16[128,128]{1,0:T(8,128)(2,1)}, bf16[128,128]{1,0:T(8,128)(2,1)}) custom-call(bf16[128,512]{1,0:T(8,128)(2,1)S(1)} %copy-done.7, bf16[128,512]{1,0:T(8,128)(2,1)} %copy-done.15, bf16[128,512]{1,0:T(8,128)(2,1)} %copy-done.16, bf16[128,512]{1,0:T(8,128)(2,1)} %copy-done.17), custom_call_target="tpu_custom_call" | custom-call | bytes 4000000 | tf_op jit(solution)/shard_map/pallas_call | solution.py:404
  (51 shorter events, 5.1 us)
Async XLA Ops:
  3.6 5.2 %copy-start.3 = (bf16[1,128,1024]{2,1,0:T(8,128)(2,1)S(1)}, bf16[1,128,1024]{2,1,0:T(8,128)(2,1)}, u32[]{:S(2)}) copy-start(bf16[1,128,1024]{2,1,0:T(8,128)(2,1)} %param.9) | copy-start | bytes 786436
  3.6 5.2 %copy-start.4 = (bf16[1,128,1024]{2,1,0:T(8,128)(2,1)S(1)}, bf16[1,128,1024]{2,1,0:T(8,128)(2,1)}, u32[]{:S(2)}) copy-start(bf16[1,128,1024]{2,1,0:T(8,128)(2,1)} %param.12) | copy-start | bytes 786436
  3.6 5.2 %copy-start.8 = (bf16[1,128,128]{2,1,0:T(8,128)(2,1)S(1)}, bf16[1,128,128]{2,1,0:T(8,128)(2,1)}, u32[]{:S(2)}) copy-start(bf16[1,128,128]{2,1,0:T(8,128)(2,1)} %param.10) | copy-start | bytes 98308
  3.6 5.2 %copy-start.9 = (bf16[1,128,128]{2,1,0:T(8,128)(2,1)S(1)}, bf16[1,128,128]{2,1,0:T(8,128)(2,1)}, u32[]{:S(2)}) copy-start(bf16[1,128,128]{2,1,0:T(8,128)(2,1)} %param.11) | copy-start | bytes 98308
  3.6 17.5 %copy-start.2 = (bf16[4096,16]{0,1:T(8,128)(2,1)S(1)}, bf16[4096,16]{0,1:T(8,128)(2,1)}, u32[]{:S(2)}) copy-start(bf16[4096,16]{0,1:T(8,128)(2,1)} %param.13) | copy-start | bytes 393220
  3.6 17.5 %copy-start.10 = (f32[16]{0:T(128)S(1)}, f32[16]{0:T(128)}, u32[]{:S(2)}) copy-start(f32[16]{0:T(128)} %param.14) | copy-start | bytes 196
  3.6 17.5 %all-to-all-start = ((bf16[4,144,1024]{2,1,0:T(8,128)(2,1)}), bf16[4,144,1024]{2,1,0:T(8,128)(2,1)S(1)}, u32[]{:S(2)}, u32[]{:S(2)}) async-start(bf16[4,144,1024]{2,1,0:T(8,128)(2,1)} %shard_map.119), calls=%async_computation | async-start | bytes 2359296 | tf_op jit(solution)/shard_map/all_to_all | solution.py:453
  8.8 26.7 %copy-start.11 = (f32[16]{0:T(128)S(1)}, f32[16]{0:T(128)}, u32[]{:S(2)}) copy-start(f32[16]{0:T(128)} %param.15) | copy-start | bytes 196
  9.9 25.6 %copy-start.6 = (bf16[128,768]{1,0:T(8,128)(2,1)S(1)}, bf16[128,768]{1,0:T(8,128)(2,1)}, u32[]{:S(2)}) copy-start(bf16[128,768]{1,0:T(8,128)(2,1)} %get-tuple-element.25.refs_0_) | copy-start | bytes 589828
  9.9 21.2 %collective-permute-start = (bf16[128,768]{1,0:T(8,128)(2,1)}, bf16[128,768]{1,0:T(8,128)(2,1)S(1)}, u32[]{:S(2)}, u32[]{:S(2)}) collective-permute-start(bf16[128,768]{1,0:T(8,128)(2,1)} %get-tuple-element.26), channel_id=1, source_target_pairs={{0,16},{16,32},{32,48},{48,0},{64,80},{80,96},{96,112},{112,64},{1... | collective-permute-start | bytes 589832 | tf_op jit(solution)/shard_map/ppermute | solution.py:444
  13.6 17.5 %collective-permute-start.1 = (bf16[128,768]{1,0:T(8,128)(2,1)}, bf16[128,768]{1,0:T(8,128)(2,1)S(1)}, u32[]{:S(2)}, u32[]{:S(2)}) collective-permute-start(bf16[128,768]{1,0:T(8,128)(2,1)} %get-tuple-element.27), channel_id=1, source_target_pairs={{0,32},{16,48},{32,0},{48,16},{64,96},{80,112},{96,64},{112,80},{1... | collective-permute-start | bytes 589832 | tf_op jit(solution)/shard_map/ppermute | solution.py:444
  18.5 13.9 %collective-permute-start.2 = (bf16[128,768]{1,0:T(8,128)(2,1)}, bf16[128,768]{1,0:T(8,128)(2,1)S(1)}, u32[]{:S(2)}, u32[]{:S(2)}) collective-permute-start(bf16[128,768]{1,0:T(8,128)(2,1)} %get-tuple-element.28), channel_id=1, source_target_pairs={{0,48},{16,0},{32,16},{48,32},{64,112},{80,64},{96,80},{112,96},{1... | collective-permute-start | bytes 589832 | tf_op jit(solution)/shard_map/ppermute | solution.py:444
  21.1 44.1 %copy-start = (bf16[4,144,1024]{2,1,0:T(8,128)(2,1)}, bf16[4,144,1024]{2,1,0:T(8,128)(2,1)S(1)}, u32[]{:S(2)}) copy-start(bf16[4,144,1024]{2,1,0:T(8,128)(2,1)S(1)} %all-to-all-done.whole_ref) | copy-start | bytes 3538948
  22.2 13.4 %all-to-all-start.1 = ((f32[4,4,128]{2,1,0:T(4,128)}), f32[4,4,128]{2,1,0:T(4,128)S(1)}, u32[]{:S(2)}, u32[]{:S(2)}) async-start(f32[4,4,128]{2,1,0:T(4,128)} %shard_map.120), calls=%async_computation.1 | async-start | bytes 16384 | tf_op jit(solution)/shard_map/all_to_all | solution.py:416
  65.9 17.1 %all-to-all-start.3 = ((bf16[8,64,128]{2,1,0:T(8,128)(2,1)}), bf16[8,64,128]{2,1,0:T(8,128)(2,1)S(1)}, u32[]{:S(2)}, u32[]{:S(2)}) async-start(bf16[8,64,128]{2,1,0:T(8,128)(2,1)} %shard_map.123), calls=%async_computation.3 | async-start | bytes 262144 | tf_op jit(solution)/shard_map/all_to_all | solution.py:416
  85.1 28.9 %copy-start.20 = (bf16[128,512]{1,0:T(8,128)(2,1)S(1)}, bf16[128,512]{1,0:T(8,128)(2,1)}, u32[]{:S(2)}) copy-start(bf16[128,512]{1,0:T(8,128)(2,1)} %get-tuple-element.38) | copy-start | bytes 393220
  85.1 32.2 %copy-start.19 = (bf16[128,512]{1,0:T(8,128)(2,1)S(1)}, bf16[128,512]{1,0:T(8,128)(2,1)}, u32[]{:S(2)}) copy-start(bf16[128,512]{1,0:T(8,128)(2,1)} %get-tuple-element.39) | copy-start | bytes 393220
  85.1 36.2 %copy-start.18 = (bf16[128,512]{1,0:T(8,128)(2,1)S(1)}, bf16[128,512]{1,0:T(8,128)(2,1)}, u32[]{:S(2)}) copy-start(bf16[128,512]{1,0:T(8,128)(2,1)} %get-tuple-element.40) | copy-start | bytes 393220
  103.3 29.2 %copy-start.7 = (bf16[128,512]{1,0:T(8,128)(2,1)S(1)}, bf16[128,512]{1,0:T(8,128)(2,1)}, u32[]{:S(2)}) copy-start(bf16[128,512]{1,0:T(8,128)(2,1)} %get-tuple-element.37.refs_0_) | copy-start | bytes 393220
  103.3 31.0 %all-to-all-start.5 = ((bf16[128,4,128]{2,1,0:T(4,128)(2,1)}), bf16[128,4,128]{2,1,0:T(4,128)(2,1)S(1)}, u32[]{:S(2)}, u32[]{:S(2)}) async-start(bf16[128,4,128]{2,1,0:T(4,128)(2,1)} %shard_map.128), calls=%async_computation.5 | async-start | bytes 262144 | tf_op jit(solution)/shard_map/all_to_all | solution.py:416
  114.0 12.6 %collective-permute-start.3 = (bf16[128,512]{1,0:T(8,128)(2,1)S(1)}, bf16[128,512]{1,0:T(8,128)(2,1)S(1)}, u32[]{:S(2)}, u32[]{:S(2)}) collective-permute-start(bf16[128,512]{1,0:T(8,128)(2,1)S(1)} %copy-done.20), channel_id=1, source_target_pairs={{0,16},{16,32},{32,48},{48,0},{64,80},{80,96},{96,112},{112,64},{1... | collective-permute-start | bytes 393224 | tf_op jit(solution)/shard_map/ppermute | solution.py:444
  117.3 14.5 %collective-permute-start.4 = (bf16[128,512]{1,0:T(8,128)(2,1)S(1)}, bf16[128,512]{1,0:T(8,128)(2,1)S(1)}, u32[]{:S(2)}, u32[]{:S(2)}) collective-permute-start(bf16[128,512]{1,0:T(8,128)(2,1)S(1)} %copy-done.19), channel_id=1, source_target_pairs={{0,32},{16,48},{32,0},{48,16},{64,96},{80,112},{96,64},{112,80},{1... | collective-permute-start | bytes 393224 | tf_op jit(solution)/shard_map/ppermute | solution.py:444
  121.3 10.5 %collective-permute-start.5 = (bf16[128,512]{1,0:T(8,128)(2,1)S(1)}, bf16[128,512]{1,0:T(8,128)(2,1)S(1)}, u32[]{:S(2)}, u32[]{:S(2)}) collective-permute-start(bf16[128,512]{1,0:T(8,128)(2,1)S(1)} %copy-done.18), channel_id=1, source_target_pairs={{0,48},{16,0},{32,16},{48,32},{64,112},{80,64},{96,80},{112,96},{1... | collective-permute-start | bytes 393224 | tf_op jit(solution)/shard_map/ppermute | solution.py:444
  126.6 5.2 %copy-start.15 = (bf16[128,512]{1,0:T(8,128)(2,1)}, bf16[128,512]{1,0:T(8,128)(2,1)S(1)}, u32[]{:S(2)}) copy-start(bf16[128,512]{1,0:T(8,128)(2,1)S(1)} %collective-permute-done.3.refs_1_) | copy-start | bytes 393220
  (7 other events, 15.2 us)

commit v4 on v3

--- a/solution.py
+++ b/solution.py
@@ -107,13 +107,16 @@
 
 def state_kernel(terms_ref, log_ref, *refs):
     received = refs[:NEAR]
-    sent_ref, data_ref, small_ref, states_ref, scaled_ref = refs[NEAR:]
+    sent_ref, data_ref, small_ref, states_ref, scaled_ref, arrived = refs[NEAR:]
     each, tokens = terms_ref.shape[1:]
     rows = NEAR * each
     wide = each * P_SIZE
     place = lax.rem(lax.axis_index("seq"), NEAR)
+    copies = []
     for shift in range(NEAR):
-        data_ref[lax.rem(place + NEAR - shift, NEAR)] = received[shift][...]
+        to = data_ref.at[lax.rem(place + NEAR - shift, NEAR)]
+        copies.append(pltpu.make_async_copy(received[shift], to, arrived.at[shift]))
+        copies[-1].start()
     preact = jnp.concatenate([terms_ref[at] for at in range(NEAR)], axis=0)
     tail = jnp.exp(-jnp.abs(preact))
     step = jnp.maximum(preact, 0.0) + jnp.log1p(tail)
@@ -127,6 +130,8 @@
     small_ref[3] = jnp.broadcast_to(rate, cumulated.shape)
     inflow = halves(jnp.transpose(jnp.exp(total - cumulated) * step))
     since = halves(jnp.transpose(jnp.exp(cumulated)))
+    for copy in copies:
+        copy.wait()
     for at in range(NEAR):
         segments = segment_matrix(rows, each, at)
         x, g, b, c = views(data_ref, at, wide)
@@ -224,11 +229,15 @@
 
 
 def last_kernel(
-    far_ref, data_ref, small_ref, states_ref, scaled_ref, inner_ref, pair_ref,
-    sums_ref, *refs
+    far_ref, data_ref, small_ref, states_ref, scaled_ref, inner_ref, pairs_ref,
+    sums_ref, kept_ref, *refs
 ):
     own_refs = refs[:NEAR]
-    pre_ref, result_ref = refs[NEAR:]
+    pre_ref, whole_ref, result_ref, pair_ref, arrived = refs[NEAR:]
+    pairs = pltpu.make_async_copy(pairs_ref, pair_ref, arrived.at[0])
+    pairs.start()
+    fetch = pltpu.make_async_copy(kept_ref, whole_ref, arrived.at[1])
+    fetch.start()
     _, rows, tokens = small_ref.shape
     each = rows // NEAR
     wide = each * P_SIZE
@@ -274,12 +283,6 @@
             spread(step_halves, segments)
             * (inner_ref[at].astype(F32) + spread(left_halves, segments) * from_grad)
         ).astype(BF16)
-        result_ref[at, :, wide : wide + NSTATE] = (
-            pair_ref[0, at].astype(F32) + dot(scaled_ref[0, at], grad, 1, 0)
-        ).astype(BF16)
-        result_ref[at, :, wide + NSTATE :] = (
-            pair_ref[1, at].astype(F32) + dot(scaled_ref[1, at], state, 1, 0)
-        ).astype(BF16)
         from_inflow = from_inflow + gathered(x.astype(F32) * from_grad, segments)
         from_readout = from_readout + gathered(g.astype(F32) * from_state, segments)
         high, low = halves(coming[at] * leaving[at])
@@ -300,8 +303,17 @@
         rounded = grad_pre[at * each : (at + 1) * each].astype(BF16)
         for part in range(parts):
             pre_ref[at * parts + part] = rounded
+    pairs.wait()
+    for at in range(NEAR):
+        for which, of_state in ((0, leaving[at]), (1, coming[at])):
+            first = wide + which * NSTATE
+            result_ref[at, :, first : first + NSTATE] = (
+                pair_ref[which, at].astype(F32)
+                + dot(scaled_ref[which, at], of_state.astype(BF16), 1, 0)
+            ).astype(BF16)
     for shift in range(NEAR):
         own_refs[shift][...] = result_ref[lax.rem(place + shift, NEAR)]
+    fetch.wait()
 
 
 def part_kernel(pre_ref, whole_ref, part_ref):
@@ -398,9 +410,12 @@
     return pltpu.with_memory_space_constraint(value, pltpu.VMEM)
 
 
-def call(kernel, out_shape, *args, scratch=()):
+def call(kernel, out_shape, *args, scratch=(), far={}):
     cost = pl.CostEstimate(flops=0, transcendentals=0, bytes_accessed=4_000_000)
-    specs = [pl.BlockSpec(memory_space=pltpu.VMEM)] * len(args)
+    specs = [
+        pl.BlockSpec(memory_space=far.get(index, pltpu.VMEM))
+        for index in range(len(args))
+    ]
     return pl.pallas_call(
         kernel, out_shape=out_shape, in_specs=specs, scratch_shapes=scratch,
         cost_estimate=cost,
@@ -441,14 +456,15 @@
             for run in range(runs)
             for at in range(NEAR)
         ]
-        return outside(lax.ppermute(value, "seq", pairs))
+        return lax.ppermute(value, "seq", pairs)
 
     x, b, c, g = head_input[0], in_matrix[0], out_matrix[0], grad_output[0]
     bias = step_bias.reshape(1, heads)
     logs = decay_log.reshape(1, heads)
     weight = step_weight.T
     packed = call(
-        pack_kernel, shape((parts, tokens + heads, width), BF16), layer_input[0], weight
+        pack_kernel, shape((parts, tokens + heads, width), BF16),
+        outside(layer_input[0]), outside(weight),
     )
     whole = lax.all_to_all(packed, "head", 0, 0, tiled=True)
     kept = outside(whole)
@@ -457,7 +473,8 @@
         (shape((tokens, 2 * wide + 2 * NSTATE), BF16),) * NEAR,
         x, g, b, c,
     )
-    received = [data[0]] + [turn(data[shift], shift) for shift in range(1, NEAR)]
+    received = [outside(data[0])]
+    received += [outside(turn(data[shift], shift)) for shift in range(1, NEAR)]
     terms = call(preact_kernel, local((NEAR, each, tokens), F32), whole, weight, bias)
     terms = exchange(terms, "seq", near)
     sent, data, small, states, scaled = call(
@@ -469,37 +486,44 @@
             local((2, NEAR, wide, NSTATE), BF16),
             local((2, NEAR, tokens, wide), BF16),
         ),
-        terms, logs, *received,
+        terms, logs, *received, far={index: pltpu.HBM for index in range(2, 2 + NEAR)},
+        scratch=(pltpu.SemaphoreType.DMA((NEAR,)),),
     )
     sent = exchange(sent, "seq", far)
     inner, pair, sums = call(
         inner_kernel,
         (
             local((NEAR, tokens, wide), BF16),
-            local((2, NEAR, tokens, NSTATE), BF16),
+            shape((2, NEAR, tokens, NSTATE), BF16),
             local((2, rows, tokens), F32),
         ),
         data, small,
     )
     back = call(far_kernel, local((runs, 2 * wide // runs, NSTATE), BF16), sent)
     back = exchange(back, "seq", far)
-    *owned, pre = call(
+    *owned, pre, whole = call(
         last_kernel,
-        (shape((tokens, wide + 2 * NSTATE), BF16),) * NEAR + (local((count, each, tokens), BF16),),
-        back, data, small, states, scaled, inner, pair, sums,
-        scratch=(pltpu.VMEM((NEAR, tokens, wide + 2 * NSTATE), BF16),),
+        (shape((tokens, wide + 2 * NSTATE), BF16),) * NEAR + (
+            local((count, each, tokens), BF16), local(whole.shape, BF16),
+        ),
+        back, data, small, states, scaled, inner, outside(pair), sums, kept, far={6: pltpu.HBM, 8: pltpu.HBM},
+        scratch=(
+            pltpu.VMEM((NEAR, tokens, wide + 2 * NSTATE), BF16),
+            pltpu.VMEM(pair.shape, BF16),
+            pltpu.SemaphoreType.DMA((2,)),
+        ),
     )
     pre = exchange(pre, ("seq", "head"), block)
     part = call(
         part_kernel,
         local((places * shards, heads // shards, LANES), BF16),
-        pre, kept,
+        pre, whole,
     )
     part = exchange(part, ("seq", "dp"))
     returned = [owned[0]]
     for shift in range(1, NEAR):
         returned.append(turn(owned[shift], shift))
-    grad_input = call(input_kernel, shape((tokens, width), BF16), pre, kept)
+    grad_input = call(input_kernel, shape((tokens, width), BF16), pre, whole)
     grad_x, grad_b, grad_c = call(
         final_kernel,
         (shape(x.shape, BF16), shape(b.shape, BF16), shape(c.shape, BF16)),

time: 137 us -> 134 us (0.978)
  local copies, waits for them, and re-layouts: 2.62 us -> 0.06 us
    unnamed x42 -> x30, local copies, waits for them, and re-layouts: 2.62 us -> 0.06 us
  transfers between devices with their start and end apart: 10 -> 10, of which waited for: 4 -> 5; matrix products, arithmetic and copies ran while one was open for 0% -> 0% of each run, Pallas kernels for 6% -> 5%
where the time goes in v4:
time: 134 us; the launch traced here: 132 us
  starting transfers between devices  50.6 us (38%)
  blocking collectives  41.6 us (31%)
  waiting for transfers between devices  21.2 us (16%)
  Pallas kernels  17.8 us (13%)
    all_to_all x2, blocking collectives, exchange(): lax.all_to_all(value, axis, 0, 0, tiled=True, axis_index_groups=groups)  41.6 us
    all_to_all x3, starting transfers between devices, exchange(): lax.all_to_all(value, axis, 0, 0, tiled=True, axis_index_groups=groups)  24.1 us
    ppermute x6, starting transfers between devices, turn(): return lax.ppermute(value, 'seq', pairs)  21.4 us
    pallas_call x11, Pallas kernels, call(): pl.pallas_call(kernel, out_shape=out_shape, in_specs=specs, scratch_shape...  17.8 us
    all_to_all x3, waiting for transfers between devices, exchange(): lax.all_to_all(value, axis, 0, 0, tiled=True, axis_index_groups=groups)  13.5 us
    ppermute x6, waiting for transfers between devices, turn(): return lax.ppermute(value, 'seq', pairs)  7.66 us
    all_to_all x1, starting transfers between devices, body(): whole = lax.all_to_all(packed, 'head', 0, 0, tiled=True)  5.14 us
  transfers between devices with their start and end apart: 10, of which 5 were waited for; matrix products, arithmetic and copies ran while one was open for 0% of the time, Pallas kernels for 5%

profile of v4, /device:TPU:1, one launch (start us, length us, event | category | flops | bytes accessed | tf_op | source)
XLA Modules:
  0.0 132.2 jit_solution(12478123639836103833)
XLA Ops:
  0.6 2.1 %shard_map.119 = bf16[4,144,1024]{2,1,0:T(8,128)(2,1)} custom-call(bf16[128,1024]{1,0:T(8,128)(2,1)} %bitcast.21, bf16[16,4096]{1,0:T(8,128)(2,1)} %bitcast.13), custom_call_target="tpu_custom_call" | custom-call | bytes 4000000 | tf_op jit(solution)/shard_map/pallas_call | solution.py:419
  2.8 5.1 %all-to-all-start = ((bf16[4,144,1024]{2,1,0:T(8,128)(2,1)}), bf16[4,144,1024]{2,1,0:T(8,128)(2,1)S(1)}, u32[]{:S(2)}, u32[]{:S(2)}) async-start(bf16[4,144,1024]{2,1,0:T(8,128)(2,1)} %shard_map.119), calls=%async_computation | async-start | bytes 2359296 | tf_op jit(solution)/shard_map/all_to_all | solution.py:469
  7.9 1.1 shard_map.121
  9.0 3.5 %collective-permute-start = (bf16[128,768]{1,0:T(8,128)(2,1)}, bf16[128,768]{1,0:T(8,128)(2,1)S(1)}, u32[]{:S(2)}, u32[]{:S(2)}) collective-permute-start(bf16[128,768]{1,0:T(8,128)(2,1)} %get-tuple-element.27), channel_id=1, source_target_pairs={{0,16},{16,32},{32,48},{48,0},{64,80},{80,96},{96,112},{112,64},{1... | collective-permute-start | bytes 589832 | tf_op jit(solution)/shard_map/ppermute | solution.py:459
  12.5 4.9 %collective-permute-start.1 = (bf16[128,768]{1,0:T(8,128)(2,1)}, bf16[128,768]{1,0:T(8,128)(2,1)S(1)}, u32[]{:S(2)}, u32[]{:S(2)}) collective-permute-start(bf16[128,768]{1,0:T(8,128)(2,1)} %get-tuple-element.28), channel_id=1, source_target_pairs={{0,32},{16,48},{32,0},{48,16},{64,96},{80,112},{96,64},{112,80},{1... | collective-permute-start | bytes 589832 | tf_op jit(solution)/shard_map/ppermute | solution.py:459
  17.4 2.6 %collective-permute-start.2 = (bf16[128,768]{1,0:T(8,128)(2,1)}, bf16[128,768]{1,0:T(8,128)(2,1)S(1)}, u32[]{:S(2)}, u32[]{:S(2)}) collective-permute-start(bf16[128,768]{1,0:T(8,128)(2,1)} %get-tuple-element.29), channel_id=1, source_target_pairs={{0,48},{16,0},{32,16},{48,32},{64,112},{80,64},{96,80},{112,96},{1... | collective-permute-start | bytes 589832 | tf_op jit(solution)/shard_map/ppermute | solution.py:459
  20.1 1.0 shard_map.120
  21.1 9.1 %all-to-all-start.1 = ((f32[4,4,128]{2,1,0:T(4,128)}), f32[4,4,128]{2,1,0:T(4,128)S(1)}, u32[]{:S(2)}, u32[]{:S(2)}) async-start(f32[4,4,128]{2,1,0:T(4,128)} %shard_map.120), calls=%async_computation.1 | async-start | bytes 16384 | tf_op jit(solution)/shard_map/all_to_all | solution.py:431
  30.2 1.2 collective-permute-done.2.refs_3_
  31.4 3.2 %all-to-all-done.1.terms_ref = f32[4,4,128]{2,1,0:T(4,128)S(1)} async-done(((f32[4,4,128]{2,1,0:T(4,128)}), f32[4,4,128]{2,1,0:T(4,128)S(1)}, u32[]{:S(2)}, u32[]{:S(2)}) %all-to-all-start.1) | async-done | bytes 8224 | tf_op jit(solution)/shard_map/all_to_all | solution.py:431
  34.6 3.5 %shard_map.122 = (bf16[8,80,128]{2,1,0:T(8,128)(2,1)S(1)}, bf16[4,128,768]{2,1,0:T(8,128)(2,1)S(1)}, f32[4,16,128]{2,1,0:T(8,128)S(1)}, bf16[2,4,256,128]{3,2,1,0:T(8,128)(2,1)S(1)}, bf16[2,4,128,256]{3,2,1,0:T(8,128)(2,1)S(1)}) custom-call(f32[4,4,128]{2,1,0:T(4,128)S(1)} %all-to-all-done.1.terms_ref, f32[1,16]{1,0:T(1,128)S(1)} %bitcast.20, ...), custom_call_target="tpu_custom_call" | custom-call | bytes 4000000 | tf_op jit(solution)/shard_map/pallas_call | solution.py:419
  38.2 26.0 %all_to_all.30.states_ref = bf16[8,80,128]{2,1,0:T(8,128)(2,1)S(1)} all-to-all(bf16[8,80,128]{2,1,0:T(8,128)(2,1)S(1)} %get-tuple-element.30), channel_id=1, replica_groups={{0,64,128,192,256,320,384,448},{16,80,144,208,272,336,400,464},{32,96,1..., dimensions={0} | all-to-all | bytes 327680 | tf_op jit(solution)/shard_map/all_to_all | solution.py:431
  64.9 4.4 %all-to-all-start.3 = ((bf16[8,64,128]{2,1,0:T(8,128)(2,1)}), bf16[8,64,128]{2,1,0:T(8,128)(2,1)S(1)}, u32[]{:S(2)}, u32[]{:S(2)}) async-start(bf16[8,64,128]{2,1,0:T(8,128)(2,1)} %shard_map.123), calls=%async_computation.3 | async-start | bytes 262144 | tf_op jit(solution)/shard_map/all_to_all | solution.py:431
  69.3 2.6 %shard_map.124 = (bf16[4,128,256]{2,1,0:T(8,128)(2,1)S(1)}, bf16[2,4,128,128]{3,2,1,0:T(8,128)(2,1)}, f32[2,16,128]{2,1,0:T(8,128)S(1)}) custom-call(bf16[4,128,768]{2,1,0:T(8,128)(2,1)S(1)} %get-tuple-element.31.data_ref, f32[4,16,128]{2,1,0:T(8,128)S(1)} %get-tuple-element.32.small_ref), custom_call_target="tpu_custom_call" | custom-call | bytes 4000000 | tf_op jit(solution)/shard_map/pallas_call | solution.py:419
  71.9 10.3 %all-to-all-done.3.far_ref = bf16[8,64,128]{2,1,0:T(8,128)(2,1)S(1)} async-done(((bf16[8,64,128]{2,1,0:T(8,128)(2,1)}), bf16[8,64,128]{2,1,0:T(8,128)(2,1)S(1)}, u32[]{:S(2)}, u32[]{:S(2)}) %all-to-all-start.3) | async-done | bytes 131104 | tf_op jit(solution)/shard_map/all_to_all | solution.py:431
  82.1 3.1 %shard_map.125 = (bf16[128,512]{1,0:T(8,128)(2,1)}, bf16[128,512]{1,0:T(8,128)(2,1)}, bf16[128,512]{1,0:T(8,128)(2,1)}, bf16[128,512]{1,0:T(8,128)(2,1)}, bf16[1...) custom-call(bf16[8,64,128]{2,1,0:T(8,128)(2,1)S(1)} %all-to-all-done.3.far_ref, ...), custom_call_target="tpu_custom_call" | custom-call | bytes 4000000 | tf_op jit(solution)/shard_map/pallas_call | solution.py:419
  85.2 15.6 %all_to_all.31.pre_ref = bf16[16,4,128]{2,1,0:T(4,128)(2,1)S(1)} all-to-all(bf16[16,4,128]{2,1,0:T(4,128)(2,1)S(1)} %get-tuple-element.45), channel_id=1, replica_groups={{0,4,8,12,16,20,24,28,32,36,40,44,48,52,56,60},{64,68,72,76,80,84,88,92..., dimensions={0} | all-to-all | bytes 32768 | tf_op jit(solution)/shard_map/all_to_all | solution.py:431
  100.9 1.2 shard_map.128
  102.1 10.6 %all-to-all-start.5 = ((bf16[128,4,128]{2,1,0:T(4,128)(2,1)}), bf16[128,4,128]{2,1,0:T(4,128)(2,1)S(1)}, u32[]{:S(2)}, u32[]{:S(2)}) async-start(bf16[128,4,128]{2,1,0:T(4,128)(2,1)} %shard_map.128), calls=%async_computation.5 | async-start | bytes 262144 | tf_op jit(solution)/shard_map/all_to_all | solution.py:431
  112.7 3.3 %collective-permute-start.3 = (bf16[128,512]{1,0:T(8,128)(2,1)S(1)}, bf16[128,512]{1,0:T(8,128)(2,1)S(1)}, u32[]{:S(2)}, u32[]{:S(2)}) collective-permute-start(bf16[128,512]{1,0:T(8,128)(2,1)S(1)} %copy-done.14), channel_id=1, source_target_pairs={{0,16},{16,32},{32,48},{48,0},{64,80},{80,96},{96,112},{112,64},{1... | collective-permute-start | bytes 393224 | tf_op jit(solution)/shard_map/ppermute | solution.py:459
  116.0 4.0 %collective-permute-start.4 = (bf16[128,512]{1,0:T(8,128)(2,1)S(1)}, bf16[128,512]{1,0:T(8,128)(2,1)S(1)}, u32[]{:S(2)}, u32[]{:S(2)}) collective-permute-start(bf16[128,512]{1,0:T(8,128)(2,1)S(1)} %copy-done.13), channel_id=1, source_target_pairs={{0,32},{16,48},{32,0},{48,16},{64,96},{80,112},{96,64},{112,80},{1... | collective-permute-start | bytes 393224 | tf_op jit(solution)/shard_map/ppermute | solution.py:459
  120.0 3.1 %collective-permute-start.5 = (bf16[128,512]{1,0:T(8,128)(2,1)S(1)}, bf16[128,512]{1,0:T(8,128)(2,1)S(1)}, u32[]{:S(2)}, u32[]{:S(2)}) collective-permute-start(bf16[128,512]{1,0:T(8,128)(2,1)S(1)} %copy-done.12), channel_id=1, source_target_pairs={{0,48},{16,0},{32,16},{48,32},{64,112},{80,64},{96,80},{112,96},{1... | collective-permute-start | bytes 393224 | tf_op jit(solution)/shard_map/ppermute | solution.py:459
  124.1 1.0 collective-permute-done.3.refs_1_
  125.0 5.5 %collective-permute-done.4.refs_2_ = bf16[128,512]{1,0:T(8,128)(2,1)S(1)} collective-permute-done((bf16[128,512]{1,0:T(8,128)(2,1)S(1)}, bf16[128,512]{1,0:T(8,128)(2,1)S(1)}, u32[]{:S(2)}, u32[]{:S(2)}) %collective-permute-start.4) | collective-permute-done | bytes 131104 | tf_op jit(solution)/shard_map/ppermute | solution.py:459
  (39 shorter events, 3.4 us)
Async XLA Ops:
  2.7 5.2 %copy-start.2 = (bf16[1,128,1024]{2,1,0:T(8,128)(2,1)S(1)}, bf16[1,128,1024]{2,1,0:T(8,128)(2,1)}, u32[]{:S(2)}) copy-start(bf16[1,128,1024]{2,1,0:T(8,128)(2,1)} %param.9) | copy-start | bytes 786436
  2.7 5.2 %copy-start.3 = (bf16[1,128,1024]{2,1,0:T(8,128)(2,1)S(1)}, bf16[1,128,1024]{2,1,0:T(8,128)(2,1)}, u32[]{:S(2)}) copy-start(bf16[1,128,1024]{2,1,0:T(8,128)(2,1)} %param.12) | copy-start | bytes 786436
  2.7 5.2 %copy-start.5 = (bf16[1,128,128]{2,1,0:T(8,128)(2,1)S(1)}, bf16[1,128,128]{2,1,0:T(8,128)(2,1)}, u32[]{:S(2)}) copy-start(bf16[1,128,128]{2,1,0:T(8,128)(2,1)} %param.10) | copy-start | bytes 98308
  2.7 5.2 %copy-start.6 = (bf16[1,128,128]{2,1,0:T(8,128)(2,1)S(1)}, bf16[1,128,128]{2,1,0:T(8,128)(2,1)}, u32[]{:S(2)}) copy-start(bf16[1,128,128]{2,1,0:T(8,128)(2,1)} %param.11) | copy-start | bytes 98308
  2.7 17.4 %copy-start.1 = (bf16[4096,16]{0,1:T(8,128)(2,1)S(1)}, bf16[4096,16]{0,1:T(8,128)(2,1)}, u32[]{:S(2)}) copy-start(bf16[4096,16]{0,1:T(8,128)(2,1)} %param.13) | copy-start | bytes 393220
  2.7 17.4 %copy-start.7 = (f32[16]{0:T(128)S(1)}, f32[16]{0:T(128)}, u32[]{:S(2)}) copy-start(f32[16]{0:T(128)} %param.14) | copy-start | bytes 196
  2.8 17.3 %all-to-all-start = ((bf16[4,144,1024]{2,1,0:T(8,128)(2,1)}), bf16[4,144,1024]{2,1,0:T(8,128)(2,1)S(1)}, u32[]{:S(2)}, u32[]{:S(2)}) async-start(bf16[4,144,1024]{2,1,0:T(8,128)(2,1)} %shard_map.119), calls=%async_computation | async-start | bytes 2359296 | tf_op jit(solution)/shard_map/all_to_all | solution.py:469
  7.9 26.7 %copy-start.8 = (f32[16]{0:T(128)S(1)}, f32[16]{0:T(128)}, u32[]{:S(2)}) copy-start(f32[16]{0:T(128)} %param.15) | copy-start | bytes 196
  9.0 21.2 %collective-permute-start = (bf16[128,768]{1,0:T(8,128)(2,1)}, bf16[128,768]{1,0:T(8,128)(2,1)S(1)}, u32[]{:S(2)}, u32[]{:S(2)}) collective-permute-start(bf16[128,768]{1,0:T(8,128)(2,1)} %get-tuple-element.27), channel_id=1, source_target_pairs={{0,16},{16,32},{32,48},{48,0},{64,80},{80,96},{96,112},{112,64},{1... | collective-permute-start | bytes 589832 | tf_op jit(solution)/shard_map/ppermute | solution.py:459
  12.5 17.6 %collective-permute-start.1 = (bf16[128,768]{1,0:T(8,128)(2,1)}, bf16[128,768]{1,0:T(8,128)(2,1)S(1)}, u32[]{:S(2)}, u32[]{:S(2)}) collective-permute-start(bf16[128,768]{1,0:T(8,128)(2,1)} %get-tuple-element.28), channel_id=1, source_target_pairs={{0,32},{16,48},{32,0},{48,16},{64,96},{80,112},{96,64},{112,80},{1... | collective-permute-start | bytes 589832 | tf_op jit(solution)/shard_map/ppermute | solution.py:459
  17.4 13.9 %collective-permute-start.2 = (bf16[128,768]{1,0:T(8,128)(2,1)}, bf16[128,768]{1,0:T(8,128)(2,1)S(1)}, u32[]{:S(2)}, u32[]{:S(2)}) collective-permute-start(bf16[128,768]{1,0:T(8,128)(2,1)} %get-tuple-element.29), channel_id=1, source_target_pairs={{0,48},{16,0},{32,16},{48,32},{64,112},{80,64},{96,80},{112,96},{1... | collective-permute-start | bytes 589832 | tf_op jit(solution)/shard_map/ppermute | solution.py:459
  20.1 44.1 %copy-start = (bf16[4,144,1024]{2,1,0:T(8,128)(2,1)}, bf16[4,144,1024]{2,1,0:T(8,128)(2,1)S(1)}, u32[]{:S(2)}) copy-start(bf16[4,144,1024]{2,1,0:T(8,128)(2,1)S(1)} %all-to-all-done.whole_ref.kept_ref) | copy-start | bytes 3538948
  21.1 13.5 %all-to-all-start.1 = ((f32[4,4,128]{2,1,0:T(4,128)}), f32[4,4,128]{2,1,0:T(4,128)S(1)}, u32[]{:S(2)}, u32[]{:S(2)}) async-start(f32[4,4,128]{2,1,0:T(4,128)} %shard_map.120), calls=%async_computation.1 | async-start | bytes 16384 | tf_op jit(solution)/shard_map/all_to_all | solution.py:431
  30.2 4.4 %copy-start.9 = (bf16[128,768]{1,0:T(8,128)(2,1)}, bf16[128,768]{1,0:T(8,128)(2,1)S(1)}, u32[]{:S(2)}) copy-start(bf16[128,768]{1,0:T(8,128)(2,1)S(1)} %collective-permute-done.refs_1_) | copy-start | bytes 589828
  30.2 4.4 %copy-start.10 = (bf16[128,768]{1,0:T(8,128)(2,1)}, bf16[128,768]{1,0:T(8,128)(2,1)S(1)}, u32[]{:S(2)}) copy-start(bf16[128,768]{1,0:T(8,128)(2,1)S(1)} %collective-permute-done.1.refs_2_) | copy-start | bytes 589828
  64.9 17.2 %all-to-all-start.3 = ((bf16[8,64,128]{2,1,0:T(8,128)(2,1)}), bf16[8,64,128]{2,1,0:T(8,128)(2,1)S(1)}, u32[]{:S(2)}, u32[]{:S(2)}) async-start(bf16[8,64,128]{2,1,0:T(8,128)(2,1)} %shard_map.123), calls=%async_computation.3 | async-start | bytes 262144 | tf_op jit(solution)/shard_map/all_to_all | solution.py:431
  85.2 27.5 %copy-start.14 = (bf16[128,512]{1,0:T(8,128)(2,1)S(1)}, bf16[128,512]{1,0:T(8,128)(2,1)}, u32[]{:S(2)}) copy-start(bf16[128,512]{1,0:T(8,128)(2,1)} %get-tuple-element.39) | copy-start | bytes 393220
  85.2 30.8 %copy-start.13 = (bf16[128,512]{1,0:T(8,128)(2,1)S(1)}, bf16[128,512]{1,0:T(8,128)(2,1)}, u32[]{:S(2)}) copy-start(bf16[128,512]{1,0:T(8,128)(2,1)} %get-tuple-element.40) | copy-start | bytes 393220
  85.2 34.8 %copy-start.12 = (bf16[128,512]{1,0:T(8,128)(2,1)S(1)}, bf16[128,512]{1,0:T(8,128)(2,1)}, u32[]{:S(2)}) copy-start(bf16[128,512]{1,0:T(8,128)(2,1)} %get-tuple-element.41) | copy-start | bytes 393220
  102.1 28.5 %copy-start.4 = (bf16[128,512]{1,0:T(8,128)(2,1)S(1)}, bf16[128,512]{1,0:T(8,128)(2,1)}, u32[]{:S(2)}) copy-start(bf16[128,512]{1,0:T(8,128)(2,1)} %get-tuple-element.38.refs_0_) | copy-start | bytes 393220
  102.1 29.3 %all-to-all-start.5 = ((bf16[128,4,128]{2,1,0:T(4,128)(2,1)}), bf16[128,4,128]{2,1,0:T(4,128)(2,1)S(1)}, u32[]{:S(2)}, u32[]{:S(2)}) async-start(bf16[128,4,128]{2,1,0:T(4,128)(2,1)} %shard_map.128), calls=%async_computation.5 | async-start | bytes 262144 | tf_op jit(solution)/shard_map/all_to_all | solution.py:431
  112.7 12.3 %collective-permute-start.3 = (bf16[128,512]{1,0:T(8,128)(2,1)S(1)}, bf16[128,512]{1,0:T(8,128)(2,1)S(1)}, u32[]{:S(2)}, u32[]{:S(2)}) collective-permute-start(bf16[128,512]{1,0:T(8,128)(2,1)S(1)} %copy-done.14), channel_id=1, source_target_pairs={{0,16},{16,32},{32,48},{48,0},{64,80},{80,96},{96,112},{112,64},{1... | collective-permute-start | bytes 393224 | tf_op jit(solution)/shard_map/ppermute | solution.py:459
  116.0 14.5 %collective-permute-start.4 = (bf16[128,512]{1,0:T(8,128)(2,1)S(1)}, bf16[128,512]{1,0:T(8,128)(2,1)S(1)}, u32[]{:S(2)}, u32[]{:S(2)}) collective-permute-start(bf16[128,512]{1,0:T(8,128)(2,1)S(1)} %copy-done.13), channel_id=1, source_target_pairs={{0,32},{16,48},{32,0},{48,16},{64,96},{80,112},{96,64},{112,80},{1... | collective-permute-start | bytes 393224 | tf_op jit(solution)/shard_map/ppermute | solution.py:459
  120.0 10.5 %collective-permute-start.5 = (bf16[128,512]{1,0:T(8,128)(2,1)S(1)}, bf16[128,512]{1,0:T(8,128)(2,1)S(1)}, u32[]{:S(2)}, u32[]{:S(2)}) collective-permute-start(bf16[128,512]{1,0:T(8,128)(2,1)S(1)} %copy-done.12), channel_id=1, source_target_pairs={{0,48},{16,0},{32,16},{48,32},{64,112},{80,64},{96,80},{112,96},{1... | collective-permute-start | bytes 393224 | tf_op jit(solution)/shard_map/ppermute | solution.py:459
  (1 other events, 3.2 us)

commit v5 on v4

--- a/solution.py
+++ b/solution.py
@@ -10,7 +10,7 @@
 NSTATE = 128
 LANES = 128
 NEAR = 4
-EXTRA = 16
+EXTRA = 8
 F32 = jnp.float32
 BF16 = jnp.bfloat16
 EXACT = lax.Precision.HIGHEST
@@ -375,7 +375,8 @@
     out_ref[...] = dot(pre, weights.reshape(parts * heads, width), 0, 0).astype(BF16)
 
 
-def final_kernel(*refs):
+def final_kernel(term_ref, *refs):
+    del term_ref
     received = refs[:NEAR]
     gx_ref, gb_ref, gc_ref = refs[NEAR:]
     wide = gx_ref.shape[1] // NEAR
@@ -524,12 +525,12 @@
     for shift in range(1, NEAR):
         returned.append(turn(owned[shift], shift))
     grad_input = call(input_kernel, shape((tokens, width), BF16), pre, whole)
+    term = call(sum_kernel, shape((heads, LANES // shards), F32), part)
     grad_x, grad_b, grad_c = call(
         final_kernel,
         (shape(x.shape, BF16), shape(b.shape, BF16), shape(c.shape, BF16)),
-        *returned,
-    )
-    term = call(sum_kernel, shape((heads, LANES // shards), F32), part)
+        outside(term), *returned, far={0: pltpu.HBM},
+    )
     return (grad_x[None], grad_b[None], grad_c[None], grad_input[None], term.T)
 
 

time: 134 us -> 132 us (0.985)
    ppermute x6, waiting for transfers between devices: 7.66 us -> 2.83 us  [turn(): return lax.ppermute(value, 'seq', pairs)]
    all_to_all x3, waiting for transfers between devices: 13.5 us -> 17.3 us  [exchange(): lax.all_to_all(value, axis, 0, 0, tiled=True, axis_index_groups=groups)]
where the time goes in v5:
time: 132 us; the launch traced here: 130 us
  starting transfers between devices  50.1 us (38%)
  blocking collectives  41.5 us (31%)
  waiting for transfers between devices  20.1 us (15%)
  Pallas kernels  17.8 us (13%)
    all_to_all x2, blocking collectives, exchange(): lax.all_to_all(value, axis, 0, 0, tiled=True, axis_index_groups=groups)  41.5 us
    all_to_all x3, starting transfers between devices, exchange(): lax.all_to_all(value, axis, 0, 0, tiled=True, axis_index_groups=groups)  23.6 us
    ppermute x6, starting transfers between devices, turn(): return lax.ppermute(value, 'seq', pairs)  21.4 us
    pallas_call x11, Pallas kernels, call(): pl.pallas_call(kernel, out_shape=out_shape, in_specs=specs, scratch_shape...  17.8 us
    all_to_all x3, waiting for transfers between devices, exchange(): lax.all_to_all(value, axis, 0, 0, tiled=True, axis_index_groups=groups)  17.3 us
    all_to_all x1, starting transfers between devices, body(): whole = lax.all_to_all(packed, 'head', 0, 0, tiled=True)  5.14 us
    ppermute x6, waiting for transfers between devices, turn(): return lax.ppermute(value, 'seq', pairs)  2.83 us
  transfers between devices with their start and end apart: 10, of which 5 were waited for; matrix products, arithmetic and copies ran while one was open for 0% of the time, Pallas kernels for 5%

profile of v5, /device:TPU:1, one launch (start us, length us, event | category | flops | bytes accessed | tf_op | source)
XLA Modules:
  0.0 130.5 jit_solution(635347236437211376)
XLA Ops:
  0.6 2.1 %shard_map.119 = bf16[4,144,1024]{2,1,0:T(8,128)(2,1)} custom-call(bf16[128,1024]{1,0:T(8,128)(2,1)} %bitcast.21, bf16[16,4096]{1,0:T(8,128)(2,1)} %bitcast.13), custom_call_target="tpu_custom_call" | custom-call | bytes 4000000 | tf_op jit(solution)/shard_map/pallas_call | solution.py:420
  2.8 5.1 %all-to-all-start = ((bf16[4,144,1024]{2,1,0:T(8,128)(2,1)}), bf16[4,144,1024]{2,1,0:T(8,128)(2,1)S(1)}, u32[]{:S(2)}, u32[]{:S(2)}) async-start(bf16[4,144,1024]{2,1,0:T(8,128)(2,1)} %shard_map.119), calls=%async_computation | async-start | bytes 2359296 | tf_op jit(solution)/shard_map/all_to_all | solution.py:470
  7.9 1.1 shard_map.121
  9.0 3.5 %collective-permute-start = (bf16[128,768]{1,0:T(8,128)(2,1)}, bf16[128,768]{1,0:T(8,128)(2,1)S(1)}, u32[]{:S(2)}, u32[]{:S(2)}) collective-permute-start(bf16[128,768]{1,0:T(8,128)(2,1)} %get-tuple-element.27), channel_id=1, source_target_pairs={{0,16},{16,32},{32,48},{48,0},{64,80},{80,96},{96,112},{112,64},{1... | collective-permute-start | bytes 589832 | tf_op jit(solution)/shard_map/ppermute | solution.py:460
  12.5 4.9 %collective-permute-start.1 = (bf16[128,768]{1,0:T(8,128)(2,1)}, bf16[128,768]{1,0:T(8,128)(2,1)S(1)}, u32[]{:S(2)}, u32[]{:S(2)}) collective-permute-start(bf16[128,768]{1,0:T(8,128)(2,1)} %get-tuple-element.28), channel_id=1, source_target_pairs={{0,32},{16,48},{32,0},{48,16},{64,96},{80,112},{96,64},{112,80},{1... | collective-permute-start | bytes 589832 | tf_op jit(solution)/shard_map/ppermute | solution.py:460
  17.4 2.6 %collective-permute-start.2 = (bf16[128,768]{1,0:T(8,128)(2,1)}, bf16[128,768]{1,0:T(8,128)(2,1)S(1)}, u32[]{:S(2)}, u32[]{:S(2)}) collective-permute-start(bf16[128,768]{1,0:T(8,128)(2,1)} %get-tuple-element.29), channel_id=1, source_target_pairs={{0,48},{16,0},{32,16},{48,32},{64,112},{80,64},{96,80},{112,96},{1... | collective-permute-start | bytes 589832 | tf_op jit(solution)/shard_map/ppermute | solution.py:460
  20.1 1.0 shard_map.120
  21.1 9.1 %all-to-all-start.1 = ((f32[4,4,128]{2,1,0:T(4,128)}), f32[4,4,128]{2,1,0:T(4,128)S(1)}, u32[]{:S(2)}, u32[]{:S(2)}) async-start(f32[4,4,128]{2,1,0:T(4,128)} %shard_map.120), calls=%async_computation.1 | async-start | bytes 16384 | tf_op jit(solution)/shard_map/all_to_all | solution.py:432
  30.2 1.2 collective-permute-done.2.refs_3_
  31.4 3.2 %all-to-all-done.1.terms_ref = f32[4,4,128]{2,1,0:T(4,128)S(1)} async-done(((f32[4,4,128]{2,1,0:T(4,128)}), f32[4,4,128]{2,1,0:T(4,128)S(1)}, u32[]{:S(2)}, u32[]{:S(2)}) %all-to-all-start.1) | async-done | bytes 8224 | tf_op jit(solution)/shard_map/all_to_all | solution.py:432
  34.6 3.5 %shard_map.122 = (bf16[8,72,128]{2,1,0:T(8,128)(2,1)S(1)}, bf16[4,128,768]{2,1,0:T(8,128)(2,1)S(1)}, f32[4,16,128]{2,1,0:T(8,128)S(1)}, bf16[2,4,256,128]{3,2,1,0:T(8,128)(2,1)S(1)}, bf16[2,4,128,256]{3,2,1,0:T(8,128)(2,1)S(1)}) custom-call(f32[4,4,128]{2,1,0:T(4,128)S(1)} %all-to-all-done.1.terms_ref, f32[1,16]{1,0:T(1,128)S(1)} %bitcast.20, ...), custom_call_target="tpu_custom_call" | custom-call | bytes 4000000 | tf_op jit(solution)/shard_map/pallas_call | solution.py:420
  38.2 26.0 %all_to_all.30.states_ref = bf16[8,72,128]{2,1,0:T(8,128)(2,1)S(1)} all-to-all(bf16[8,72,128]{2,1,0:T(8,128)(2,1)S(1)} %get-tuple-element.30), channel_id=1, replica_groups={{0,64,128,192,256,320,384,448},{16,80,144,208,272,336,400,464},{32,96,1..., dimensions={0} | all-to-all | bytes 294912 | tf_op jit(solution)/shard_map/all_to_all | solution.py:432
  64.9 3.7 %all-to-all-start.3 = ((bf16[8,64,128]{2,1,0:T(8,128)(2,1)}), bf16[8,64,128]{2,1,0:T(8,128)(2,1)S(1)}, u32[]{:S(2)}, u32[]{:S(2)}) async-start(bf16[8,64,128]{2,1,0:T(8,128)(2,1)} %shard_map.123), calls=%async_computation.3 | async-start | bytes 262144 | tf_op jit(solution)/shard_map/all_to_all | solution.py:432
  68.6 2.6 %shard_map.124 = (bf16[4,128,256]{2,1,0:T(8,128)(2,1)S(1)}, bf16[2,4,128,128]{3,2,1,0:T(8,128)(2,1)}, f32[2,16,128]{2,1,0:T(8,128)S(1)}) custom-call(bf16[4,128,768]{2,1,0:T(8,128)(2,1)S(1)} %get-tuple-element.31.data_ref, f32[4,16,128]{2,1,0:T(8,128)S(1)} %get-tuple-element.32.small_ref), custom_call_target="tpu_custom_call" | custom-call | bytes 4000000 | tf_op jit(solution)/shard_map/pallas_call | solution.py:420
  71.2 10.1 %all-to-all-done.3.far_ref = bf16[8,64,128]{2,1,0:T(8,128)(2,1)S(1)} async-done(((bf16[8,64,128]{2,1,0:T(8,128)(2,1)}), bf16[8,64,128]{2,1,0:T(8,128)(2,1)S(1)}, u32[]{:S(2)}, u32[]{:S(2)}) %all-to-all-start.3) | async-done | bytes 131104 | tf_op jit(solution)/shard_map/all_to_all | solution.py:432
  81.3 3.1 %shard_map.125 = (bf16[128,512]{1,0:T(8,128)(2,1)}, bf16[128,512]{1,0:T(8,128)(2,1)}, bf16[128,512]{1,0:T(8,128)(2,1)}, bf16[128,512]{1,0:T(8,128)(2,1)}, bf16[1...) custom-call(bf16[8,64,128]{2,1,0:T(8,128)(2,1)S(1)} %all-to-all-done.3.far_ref, ...), custom_call_target="tpu_custom_call" | custom-call | bytes 4000000 | tf_op jit(solution)/shard_map/pallas_call | solution.py:420
  84.4 15.5 %all_to_all.31.pre_ref = bf16[16,4,128]{2,1,0:T(4,128)(2,1)S(1)} all-to-all(bf16[16,4,128]{2,1,0:T(4,128)(2,1)S(1)} %get-tuple-element.38), channel_id=1, replica_groups={{0,4,8,12,16,20,24,28,32,36,40,44,48,52,56,60},{64,68,72,76,80,84,88,92..., dimensions={0} | all-to-all | bytes 32768 | tf_op jit(solution)/shard_map/all_to_all | solution.py:432
  99.9 1.2 shard_map.126
  101.0 10.8 %all-to-all-start.5 = ((bf16[128,4,128]{2,1,0:T(4,128)(2,1)}), bf16[128,4,128]{2,1,0:T(4,128)(2,1)S(1)}, u32[]{:S(2)}, u32[]{:S(2)}) async-start(bf16[128,4,128]{2,1,0:T(4,128)(2,1)} %shard_map.126), calls=%async_computation.5 | async-start | bytes 262144 | tf_op jit(solution)/shard_map/all_to_all | solution.py:432
  111.9 3.3 %collective-permute-start.3 = (bf16[128,512]{1,0:T(8,128)(2,1)S(1)}, bf16[128,512]{1,0:T(8,128)(2,1)S(1)}, u32[]{:S(2)}, u32[]{:S(2)}) collective-permute-start(bf16[128,512]{1,0:T(8,128)(2,1)S(1)} %copy-done.14), channel_id=1, source_target_pairs={{0,16},{16,32},{32,48},{48,0},{64,80},{80,96},{96,112},{112,64},{1... | collective-permute-start | bytes 393224 | tf_op jit(solution)/shard_map/ppermute | solution.py:460
  115.1 4.0 %collective-permute-start.4 = (bf16[128,512]{1,0:T(8,128)(2,1)S(1)}, bf16[128,512]{1,0:T(8,128)(2,1)S(1)}, u32[]{:S(2)}, u32[]{:S(2)}) collective-permute-start(bf16[128,512]{1,0:T(8,128)(2,1)S(1)} %copy-done.13), channel_id=1, source_target_pairs={{0,32},{16,48},{32,0},{48,16},{64,96},{80,112},{96,64},{112,80},{1... | collective-permute-start | bytes 393224 | tf_op jit(solution)/shard_map/ppermute | solution.py:460
  119.2 3.1 %collective-permute-start.5 = (bf16[128,512]{1,0:T(8,128)(2,1)S(1)}, bf16[128,512]{1,0:T(8,128)(2,1)S(1)}, u32[]{:S(2)}, u32[]{:S(2)}) collective-permute-start(bf16[128,512]{1,0:T(8,128)(2,1)S(1)} %copy-done.12), channel_id=1, source_target_pairs={{0,48},{16,0},{32,16},{48,32},{64,112},{80,64},{96,80},{112,96},{1... | collective-permute-start | bytes 393224 | tf_op jit(solution)/shard_map/ppermute | solution.py:460
  123.2 4.0 %all-to-all-done.5.part_ref = bf16[128,4,128]{2,1,0:T(4,128)(2,1)S(1)} async-done(((bf16[128,4,128]{2,1,0:T(4,128)(2,1)}), bf16[128,4,128]{2,1,0:T(4,128)(2,1)S(1)}, u32[]{:S(2)}, u32[]{:S(2)}) %all-to-all-start.5) | async-done | bytes 131104 | tf_op jit(solution)/shard_map/all_to_all | solution.py:432
  128.0 1.6 %collective-permute-done.4.refs_2_ = bf16[128,512]{1,0:T(8,128)(2,1)S(1)} collective-permute-done((bf16[128,512]{1,0:T(8,128)(2,1)S(1)}, bf16[128,512]{1,0:T(8,128)(2,1)S(1)}, u32[]{:S(2)}, u32[]{:S(2)}) %collective-permute-start.4) | collective-permute-done | bytes 131104 | tf_op jit(solution)/shard_map/ppermute | solution.py:460
  (39 shorter events, 3.4 us)
Async XLA Ops:
  2.7 5.2 %copy-start.2 = (bf16[1,128,1024]{2,1,0:T(8,128)(2,1)S(1)}, bf16[1,128,1024]{2,1,0:T(8,128)(2,1)}, u32[]{:S(2)}) copy-start(bf16[1,128,1024]{2,1,0:T(8,128)(2,1)} %param.9) | copy-start | bytes 786436
  2.7 5.2 %copy-start.3 = (bf16[1,128,1024]{2,1,0:T(8,128)(2,1)S(1)}, bf16[1,128,1024]{2,1,0:T(8,128)(2,1)}, u32[]{:S(2)}) copy-start(bf16[1,128,1024]{2,1,0:T(8,128)(2,1)} %param.12) | copy-start | bytes 786436
  2.7 5.2 %copy-start.5 = (bf16[1,128,128]{2,1,0:T(8,128)(2,1)S(1)}, bf16[1,128,128]{2,1,0:T(8,128)(2,1)}, u32[]{:S(2)}) copy-start(bf16[1,128,128]{2,1,0:T(8,128)(2,1)} %param.10) | copy-start | bytes 98308
  2.7 5.2 %copy-start.6 = (bf16[1,128,128]{2,1,0:T(8,128)(2,1)S(1)}, bf16[1,128,128]{2,1,0:T(8,128)(2,1)}, u32[]{:S(2)}) copy-start(bf16[1,128,128]{2,1,0:T(8,128)(2,1)} %param.11) | copy-start | bytes 98308
  2.7 17.4 %copy-start.1 = (bf16[4096,16]{0,1:T(8,128)(2,1)S(1)}, bf16[4096,16]{0,1:T(8,128)(2,1)}, u32[]{:S(2)}) copy-start(bf16[4096,16]{0,1:T(8,128)(2,1)} %param.13) | copy-start | bytes 393220
  2.7 17.4 %copy-start.7 = (f32[16]{0:T(128)S(1)}, f32[16]{0:T(128)}, u32[]{:S(2)}) copy-start(f32[16]{0:T(128)} %param.14) | copy-start | bytes 196
  2.8 17.3 %all-to-all-start = ((bf16[4,144,1024]{2,1,0:T(8,128)(2,1)}), bf16[4,144,1024]{2,1,0:T(8,128)(2,1)S(1)}, u32[]{:S(2)}, u32[]{:S(2)}) async-start(bf16[4,144,1024]{2,1,0:T(8,128)(2,1)} %shard_map.119), calls=%async_computation | async-start | bytes 2359296 | tf_op jit(solution)/shard_map/all_to_all | solution.py:470
  7.9 26.7 %copy-start.8 = (f32[16]{0:T(128)S(1)}, f32[16]{0:T(128)}, u32[]{:S(2)}) copy-start(f32[16]{0:T(128)} %param.15) | copy-start | bytes 196
  9.0 21.2 %collective-permute-start = (bf16[128,768]{1,0:T(8,128)(2,1)}, bf16[128,768]{1,0:T(8,128)(2,1)S(1)}, u32[]{:S(2)}, u32[]{:S(2)}) collective-permute-start(bf16[128,768]{1,0:T(8,128)(2,1)} %get-tuple-element.27), channel_id=1, source_target_pairs={{0,16},{16,32},{32,48},{48,0},{64,80},{80,96},{96,112},{112,64},{1... | collective-permute-start | bytes 589832 | tf_op jit(solution)/shard_map/ppermute | solution.py:460
  12.5 17.6 %collective-permute-start.1 = (bf16[128,768]{1,0:T(8,128)(2,1)}, bf16[128,768]{1,0:T(8,128)(2,1)S(1)}, u32[]{:S(2)}, u32[]{:S(2)}) collective-permute-start(bf16[128,768]{1,0:T(8,128)(2,1)} %get-tuple-element.28), channel_id=1, source_target_pairs={{0,32},{16,48},{32,0},{48,16},{64,96},{80,112},{96,64},{112,80},{1... | collective-permute-start | bytes 589832 | tf_op jit(solution)/shard_map/ppermute | solution.py:460
  17.4 13.9 %collective-permute-start.2 = (bf16[128,768]{1,0:T(8,128)(2,1)}, bf16[128,768]{1,0:T(8,128)(2,1)S(1)}, u32[]{:S(2)}, u32[]{:S(2)}) collective-permute-start(bf16[128,768]{1,0:T(8,128)(2,1)} %get-tuple-element.29), channel_id=1, source_target_pairs={{0,48},{16,0},{32,16},{48,32},{64,112},{80,64},{96,80},{112,96},{1... | collective-permute-start | bytes 589832 | tf_op jit(solution)/shard_map/ppermute | solution.py:460
  20.1 44.1 %copy-start = (bf16[4,144,1024]{2,1,0:T(8,128)(2,1)}, bf16[4,144,1024]{2,1,0:T(8,128)(2,1)S(1)}, u32[]{:S(2)}) copy-start(bf16[4,144,1024]{2,1,0:T(8,128)(2,1)S(1)} %all-to-all-done.whole_ref.kept_ref) | copy-start | bytes 3538948
  21.1 13.5 %all-to-all-start.1 = ((f32[4,4,128]{2,1,0:T(4,128)}), f32[4,4,128]{2,1,0:T(4,128)S(1)}, u32[]{:S(2)}, u32[]{:S(2)}) async-start(f32[4,4,128]{2,1,0:T(4,128)} %shard_map.120), calls=%async_computation.1 | async-start | bytes 16384 | tf_op jit(solution)/shard_map/all_to_all | solution.py:432
  30.2 4.4 %copy-start.9 = (bf16[128,768]{1,0:T(8,128)(2,1)}, bf16[128,768]{1,0:T(8,128)(2,1)S(1)}, u32[]{:S(2)}) copy-start(bf16[128,768]{1,0:T(8,128)(2,1)S(1)} %collective-permute-done.refs_1_) | copy-start | bytes 589828
  30.2 4.4 %copy-start.10 = (bf16[128,768]{1,0:T(8,128)(2,1)}, bf16[128,768]{1,0:T(8,128)(2,1)S(1)}, u32[]{:S(2)}) copy-start(bf16[128,768]{1,0:T(8,128)(2,1)S(1)} %collective-permute-done.1.refs_2_) | copy-start | bytes 589828
  64.9 16.3 %all-to-all-start.3 = ((bf16[8,64,128]{2,1,0:T(8,128)(2,1)}), bf16[8,64,128]{2,1,0:T(8,128)(2,1)S(1)}, u32[]{:S(2)}, u32[]{:S(2)}) async-start(bf16[8,64,128]{2,1,0:T(8,128)(2,1)} %shard_map.123), calls=%async_computation.3 | async-start | bytes 262144 | tf_op jit(solution)/shard_map/all_to_all | solution.py:432
  84.3 27.5 %copy-start.14 = (bf16[128,512]{1,0:T(8,128)(2,1)S(1)}, bf16[128,512]{1,0:T(8,128)(2,1)}, u32[]{:S(2)}) copy-start(bf16[128,512]{1,0:T(8,128)(2,1)} %get-tuple-element.41) | copy-start | bytes 393220
  84.3 30.8 %copy-start.13 = (bf16[128,512]{1,0:T(8,128)(2,1)S(1)}, bf16[128,512]{1,0:T(8,128)(2,1)}, u32[]{:S(2)}) copy-start(bf16[128,512]{1,0:T(8,128)(2,1)} %get-tuple-element.42) | copy-start | bytes 393220
  84.3 34.8 %copy-start.12 = (bf16[128,512]{1,0:T(8,128)(2,1)S(1)}, bf16[128,512]{1,0:T(8,128)(2,1)}, u32[]{:S(2)}) copy-start(bf16[128,512]{1,0:T(8,128)(2,1)} %get-tuple-element.43) | copy-start | bytes 393220
  101.0 28.6 %copy-start.4 = (bf16[128,512]{1,0:T(8,128)(2,1)S(1)}, bf16[128,512]{1,0:T(8,128)(2,1)}, u32[]{:S(2)}) copy-start(bf16[128,512]{1,0:T(8,128)(2,1)} %get-tuple-element.40.refs_0_) | copy-start | bytes 393220
  101.0 26.2 %all-to-all-start.5 = ((bf16[128,4,128]{2,1,0:T(4,128)(2,1)}), bf16[128,4,128]{2,1,0:T(4,128)(2,1)S(1)}, u32[]{:S(2)}, u32[]{:S(2)}) async-start(bf16[128,4,128]{2,1,0:T(4,128)(2,1)} %shard_map.126), calls=%async_computation.5 | async-start | bytes 262144 | tf_op jit(solution)/shard_map/all_to_all | solution.py:432
  111.9 16.2 %collective-permute-start.3 = (bf16[128,512]{1,0:T(8,128)(2,1)S(1)}, bf16[128,512]{1,0:T(8,128)(2,1)S(1)}, u32[]{:S(2)}, u32[]{:S(2)}) collective-permute-start(bf16[128,512]{1,0:T(8,128)(2,1)S(1)} %copy-done.14), channel_id=1, source_target_pairs={{0,16},{16,32},{32,48},{48,0},{64,80},{80,96},{96,112},{112,64},{1... | collective-permute-start | bytes 393224 | tf_op jit(solution)/shard_map/ppermute | solution.py:460
  115.1 14.5 %collective-permute-start.4 = (bf16[128,512]{1,0:T(8,128)(2,1)S(1)}, bf16[128,512]{1,0:T(8,128)(2,1)S(1)}, u32[]{:S(2)}, u32[]{:S(2)}) collective-permute-start(bf16[128,512]{1,0:T(8,128)(2,1)S(1)} %copy-done.13), channel_id=1, source_target_pairs={{0,32},{16,48},{32,0},{48,16},{64,96},{80,112},{96,64},{112,80},{1... | collective-permute-start | bytes 393224 | tf_op jit(solution)/shard_map/ppermute | solution.py:460
  119.2 10.5 %collective-permute-start.5 = (bf16[128,512]{1,0:T(8,128)(2,1)S(1)}, bf16[128,512]{1,0:T(8,128)(2,1)S(1)}, u32[]{:S(2)}, u32[]{:S(2)}) collective-permute-start(bf16[128,512]{1,0:T(8,128)(2,1)S(1)} %copy-done.12), channel_id=1, source_target_pairs={{0,48},{16,0},{32,16},{48,32},{64,112},{80,64},{96,80},{112,96},{1... | collective-permute-start | bytes 393224 | tf_op jit(solution)/shard_map/ppermute | solution.py:460
  (1 other events, 3.2 us)
